TPU v7x, 32 devices: a whole 2x2x4 slice. The times are simulated.
32 devices in a mesh: groups: 2 (over x), ctx: 16 (over z, y, core).
Axes of the slice: x: 2, y: 2, z: 4, core: 2. Of those that a mesh axis runs over, the one named last changes fastest.
Arguments:
- queries: bfloat16 [4096, 1024], P(('groups', 'ctx')), parts along dimension 0, may hold values from -27 to 27
- keys: bfloat16 [4096, 1024], P(('groups', 'ctx')), parts along dimension 0, may hold values from -6 to 6
- values: bfloat16 [4096, 1024], P(('groups', 'ctx')), parts along dimension 0, may hold values from -6 to 6
- resid: bfloat16 [4096, 2048], P(('groups', 'ctx')), parts along dimension 0, may hold values from -6 to 6
- out_proj: bfloat16 [1024, 2048], replicated, may hold values from -0.1875 to 0.1875
- norm_gain: float32 [2048], replicated, may hold values from 0.25 to 1.75
- up_proj: bfloat16 [2048, 4096], P(None, 'ctx'), may hold values from -0.125 to 0.125
- down_proj: bfloat16 [2048, 4096], P(None, 'ctx'), may hold values from -0.09375 to 0.09375
- router: bfloat16 [2048, 2], replicated, may hold values from -0.125 to 0.125
- expert_ids: int32 [4096, 1], P(('groups', 'ctx')), parts along dimension 0, may hold values from 0 to 1; in each aligned block of 128 rows (0 to 127, 128 to 255, ...) at most 80 rows name the same one
- expert_in: bfloat16 [16, 2048, 512], P('ctx'), may hold values from -0.125 to 0.125
- expert_out: bfloat16 [16, 512, 2048], P('ctx'), may hold values from -0.09375 to 0.09375
Outputs:
- layer_out: bfloat16 [4096, 2048], P(('groups', 'ctx')), parts along dimension 0
There are 2 independent parts, one for each index of `groups`. A program takes and returns all parts, laid end to end along the dimension named above; an argument that names none is the same for every part. Nothing has to cross between parts.
Inputs may be any that keep to these rules, and one draw needn't show every extreme that they name: `expert_ids`: among the 128 tokens of one index of ctx, at most 80 name the same expert; in every draw some index of ctx has 80 tokens naming one expert.
All inputs are finite; a program needn't handle non-finite values.
Results may differ from a plain program's by a relative error of at most 0.0075.
Values may be sent and summed in bfloat16 or wider, within the bound.
No kernel may reach another device: no remote copies, remote signals or barrier semaphores. Data moves between devices by JAX's collectives and lax.ppermute only.
A program may use at most 192 MiB of HBM per device.

v0:
```python
import functools
import jax
import jax.numpy as jnp
from jax import lax
from jax.experimental import pallas as pl
from jax.experimental.pallas import tpu as pltpu
from jax.sharding import PartitionSpec as P

DH = 128
SPLIT = 8


NEG_FILL = -1e30
EPSILON = 1e-06


def from_partner(array, axis, apart):
    return lax.ppermute(array, axis, [(i, i ^ 1 << apart) for i in range(lax.axis_size(axis))])


def update_state(state, query_rows, query_offset, key_block, value_block, key_offset):
    maxima, totals, numer = state
    count_query = query_rows.shape[0]
    count_keys = key_block.shape[0]
    head_count = query_rows.shape[1] // DH
    query_heads = query_rows.reshape(count_query, head_count, DH)
    key_heads = key_block.reshape(count_keys, head_count, DH)
    value_heads = value_block.reshape(count_keys, head_count, DH)
    scores = jnp.einsum(
        "qhd,khd->hqk", query_heads, key_heads, preferred_element_type=jnp.float32
    ) * DH ** (-0.5)
    query_positions = query_offset + jnp.arange(count_query, dtype=jnp.int32)
    key_positions = key_offset + jnp.arange(count_keys, dtype=jnp.int32)
    visible = (key_positions[None, :] <= query_positions[:, None])[None]
    masked = jnp.where(visible, scores, NEG_FILL)
    new_max = jnp.maximum(maxima, jnp.max(masked, axis=2))
    weights = jnp.where(visible, jnp.exp(masked - new_max[..., None]), 0.0)
    factor = jnp.exp(maxima - new_max)
    totals = totals * factor + jnp.sum(weights, axis=2)
    numer = numer * factor[..., None] + jnp.einsum(
        "hqk,khd->hqd",
        weights.astype(jnp.bfloat16),
        value_heads,
        preferred_element_type=jnp.float32,
    )
    return (new_max, totals, numer)


def attend(query_sets, keys, values):
    head_count = keys.shape[1] // DH
    initial = []
    for query_rows, query_offset in query_sets:
        count_query = query_rows.shape[0]
        initial.append(
            (
                jnp.full((head_count, count_query), NEG_FILL, jnp.float32),
                jnp.zeros((head_count, count_query), jnp.float32),
                jnp.zeros((head_count, count_query, DH), jnp.float32),
            )
        )
    states = tuple(initial)
    key_offset = jnp.int32(0)
    key_whole = lax.all_gather(keys, "ctx", axis=0, tiled=True)
    value_whole = lax.all_gather(values, "ctx", axis=0, tiled=True)
    total_keys = key_whole.shape[0]
    step_rows = min(total_keys, 1024)
    for begin in range(0, total_keys, step_rows):
        key_block = key_whole[begin : begin + step_rows]
        value_block = value_whole[begin : begin + step_rows]
        block_offset = key_offset + begin
        query_rows, query_offset = query_sets[0]
        needed = block_offset <= query_offset + query_rows.shape[0] - 1
        updated = [
            lax.cond(
                needed,
                lambda carried, rows_now=query_rows, offset_now=query_offset, keys_now=key_block, values_now=value_block, start_now=block_offset: update_state(
                    carried, rows_now, offset_now, keys_now, values_now, start_now
                ),
                lambda carried: carried,
                states[0],
            )
        ]
        states = tuple(updated)
    results = []
    for maxima, totals, numer in states:
        result = (numer / totals[..., None]).astype(jnp.bfloat16)
        results.append(
            jnp.transpose(result, (1, 0, 2)).reshape(result.shape[1], result.shape[0] * DH)
        )
    return results


def body(
    queries,
    keys,
    values,
    resid,
    out_proj,
    norm_gain,
    up_proj,
    down_proj,
    router,
    expert_ids,
    expert_in,
    expert_out,
):
    tok_rows = queries.shape[0]
    width = resid.shape[1]
    live_count = router.shape[1]
    ctx_count = lax.axis_size("ctx")
    device_index = lax.axis_index("ctx")
    base_offset = device_index * tok_rows
    attn = attend([(queries, base_offset)], keys, values)[0]
    mixed = resid.astype(jnp.float32) + jnp.dot(attn, out_proj, preferred_element_type=jnp.float32)
    normed = (
        mixed * lax.rsqrt(jnp.mean(mixed * mixed, axis=1, keepdims=True) + EPSILON) * norm_gain
    ).astype(jnp.bfloat16)
    mlp_blocks = jnp.stack([up_proj, down_proj], 0)
    for level in range(live_count.bit_length() - 1):
        other_block = from_partner(mlp_blocks, "ctx", level)
        mlp_blocks = jnp.concatenate([mlp_blocks, other_block], axis=2)
    slots_per = max(2, 5 * tok_rows // (4 * live_count))
    chosen = expert_ids[:, 0]
    onehot = (chosen[:, None] == jnp.arange(live_count, dtype=jnp.int32)[None, :]).astype(
        jnp.bfloat16
    )
    row_iota = jnp.arange(tok_rows, dtype=jnp.int32)
    strictly_lower = (row_iota[None, :] < row_iota[:, None]).astype(jnp.bfloat16)
    counts_before = jnp.dot(strictly_lower, onehot, preferred_element_type=jnp.float32)
    slot_index = jnp.sum(onehot.astype(jnp.float32) * counts_before, axis=1).astype(jnp.int32)
    target_slot = chosen * slots_per + slot_index
    dispatch_matrix = (
        jnp.arange(live_count * slots_per, dtype=jnp.int32)[:, None] == target_slot[None, :]
    ).astype(jnp.bfloat16)
    packed = jnp.dot(dispatch_matrix, normed, preferred_element_type=jnp.float32).astype(
        jnp.bfloat16
    )
    sending = jnp.broadcast_to(
        packed.reshape(1, live_count, slots_per, width), (SPLIT, live_count, slots_per, width)
    )
    sending = sending.reshape(ctx_count, 1, slots_per, width)
    own_expert = device_index % live_count
    router_column = lax.dynamic_slice_in_dim(router, own_expert, 1, 1)
    weight_in = expert_in[0]
    weight_out = expert_out[0]
    received = lax.all_to_all(sending, "ctx", split_axis=0, concat_axis=1, tiled=True)
    rows = received.reshape(-1, width)
    expert_hidden = jax.nn.gelu(
        jnp.dot(rows, weight_in, preferred_element_type=jnp.float32)
    ).astype(jnp.bfloat16)
    mlp_hidden = jax.nn.gelu(
        jnp.dot(rows, mlp_blocks[0], preferred_element_type=jnp.float32)
    ).astype(jnp.bfloat16)
    gate = jax.nn.sigmoid(jnp.dot(rows, router_column, preferred_element_type=jnp.float32))
    produced = gate * jnp.dot(expert_hidden, weight_out, preferred_element_type=jnp.float32)
    produced = produced + lax.dot_general(
        mlp_hidden, mlp_blocks[1], (((1,), (1,)), ((), ())), preferred_element_type=jnp.float32
    )
    came_back = lax.all_to_all(
        produced.astype(jnp.bfloat16).reshape(received.shape),
        "ctx",
        split_axis=1,
        concat_axis=0,
        tiled=True,
    )
    summed = jnp.sum(
        came_back.astype(jnp.float32).reshape(SPLIT, live_count * slots_per, width), axis=0
    )
    mixture_part = lax.dot_general(
        dispatch_matrix.astype(jnp.float32),
        summed,
        (((0,), (0,)), ((), ())),
        precision=lax.Precision.HIGHEST,
        preferred_element_type=jnp.float32,
    )
    return (mixed + mixture_part).astype(jnp.bfloat16)


def swap(array, mask):
    return lax.ppermute(array, "ctx", [(i, i ^ mask) for i in range(lax.axis_size("ctx"))])


VMEM = pl.BlockSpec(memory_space=pltpu.VMEM)
SMEM = pl.BlockSpec(memory_space=pltpu.SMEM)


def call(kernel, outs, specs, flops, mib, *operands):
    return pl.pallas_call(
        kernel,
        out_shape=outs,
        in_specs=specs,
        out_specs=[VMEM] * len(outs),
        compiler_params=pltpu.CompilerParams(vmem_limit_bytes=mib * 2**20),
        cost_estimate=pl.CostEstimate(
            flops=flops,
            bytes_accessed=sum(x.size * x.dtype.itemsize for x in operands),
            transcendentals=0,
        ),
    )(*operands)


def pack_kernel(query_ref, key_ref, value_ref, out_ref):
    for head in range(out_ref.shape[0]):
        columns = slice(head * DH, (head + 1) * DH)
        for at, ref in enumerate((query_ref, key_ref, value_ref)):
            out_ref[head, :, at * DH : (at + 1) * DH] = ref[:, columns]


def attention_kernel(core_ref, own_ref, other_ref, ids_ref, out_ref):
    core = core_ref[0]
    blocks, rows, _ = own_ref.shape
    row_at = lax.broadcasted_iota(jnp.int32, (rows, rows), 0)
    column_at = lax.broadcasted_iota(jnp.int32, (rows, rows), 1)
    causal = column_at <= row_at
    also = jnp.broadcast_to(core == 1, (rows, rows))
    contract = (((1,), (1,)), ((), ()))
    id_rows = jnp.broadcast_to(
        ids_ref[...].astype(jnp.float32), (out_ref.shape[1] - rows, rows)
    ).astype(jnp.bfloat16)
    for block in range(blocks):
        query = own_ref[block, :, :DH]
        scores = []
        for ref, last_visible in ((own_ref, causal), (other_ref, also)):
            for at in range(block + 1):
                score = lax.dot_general(
                    query,
                    ref[at, :, DH : 2 * DH],
                    contract,
                    preferred_element_type=jnp.float32,
                ) * DH ** (-0.5)
                if at == block:
                    score = jnp.where(last_visible, score, NEG_FILL)
                scores.append(score)
        peak = scores[0]
        for score in scores[1:]:
            peak = jnp.maximum(peak, score)
        row_max = jnp.max(peak, axis=1, keepdims=True)
        numer = jnp.zeros((rows, DH), jnp.float32)
        summed = jnp.zeros((rows, rows), jnp.float32)
        for at, score in enumerate(scores):
            weights = jnp.exp(score - row_max)
            summed = summed + weights
            ref = own_ref if at <= block else other_ref
            numer = numer + jnp.dot(
                weights.astype(jnp.bfloat16),
                ref[at % (block + 1), :, 2 * DH :],
                preferred_element_type=jnp.float32,
            )
        totals = jnp.sum(summed, axis=1, keepdims=True)
        out_ref[block, :rows, :] = (numer / totals).astype(jnp.bfloat16)
        out_ref[block, rows:, :] = id_rows


def project_kernel(back_ref, weight_ref, resid_ref, gain_ref, mixed_ref, normed_ref):
    rows = resid_ref.shape[0]
    attn = jnp.concatenate([back_ref[head, :rows, :] for head in range(back_ref.shape[0])], axis=1)
    mixed = resid_ref[...].astype(jnp.float32) + jnp.dot(
        attn, weight_ref[...], preferred_element_type=jnp.float32
    )
    mixed_ref[...] = mixed
    scale = lax.rsqrt(jnp.mean(mixed * mixed, axis=1, keepdims=True) + EPSILON)
    normed_ref[...] = (mixed * scale * gain_ref[...]).astype(jnp.bfloat16)


def mixture_kernel(
    at_ref,
    first_ref,
    second_ref,
    back_ref,
    router_ref,
    up_a,
    up_b,
    in_a,
    in_b,
    down_a,
    down_b,
    out_a,
    out_b,
    first_out,
    second_out,
):
    rows, width = first_ref.shape
    own = at_ref[0].astype(jnp.float32)

    def is_own(shard):
        ids = back_ref[shard, rows : rows + 16, :].astype(jnp.float32)[0:1, :]
        return (jnp.transpose(jnp.broadcast_to(ids, (rows, rows)))[:, 0:1] == own).astype(jnp.float32)

    normed = jnp.concatenate([first_ref[...], second_ref[...]], axis=0)
    mine = jnp.concatenate([is_own(at_ref[1]), is_own(at_ref[2])], axis=0)
    column = jnp.where(mine > 0, router_ref[0:1, :], router_ref[1:2, :])
    logits = jnp.sum(normed.astype(jnp.float32) * column, axis=1, keepdims=True)
    gate = jax.nn.sigmoid(logits)

    def hidden(weights):
        return jax.nn.gelu(jnp.dot(normed, weights[...], preferred_element_type=jnp.float32))

    mlp_a = hidden(up_a).astype(jnp.bfloat16)
    mlp_b = hidden(up_b).astype(jnp.bfloat16)
    exp_a = jnp.where(mine > 0, hidden(in_a), 0.0).astype(jnp.bfloat16)
    exp_b = jnp.where(mine > 0, 0.0, hidden(in_b)).astype(jnp.bfloat16)
    contract = (((1,), (1,)), ((), ()))
    step = min(width, 512)
    for begin in range(0, width, step):
        span = slice(begin, begin + step)
        part = gate * (
            jnp.dot(exp_a, out_a[:, span], preferred_element_type=jnp.float32)
            + jnp.dot(exp_b, out_b[:, span], preferred_element_type=jnp.float32)
        )
        part = part + (
            lax.dot_general(mlp_a, down_a[span, :], contract, preferred_element_type=jnp.float32)
            + lax.dot_general(mlp_b, down_b[span, :], contract, preferred_element_type=jnp.float32)
        )
        part = part.astype(jnp.bfloat16)
        first_out[:, span] = part[:rows]
        second_out[:, span] = part[rows:]


def body_by_pairs(
    queries,
    keys,
    values,
    resid,
    out_proj,
    norm_gain,
    up_proj,
    down_proj,
    router,
    expert_ids,
    expert_in,
    expert_out,
):
    rows, width = resid.shape
    heads = queries.shape[1] // DH
    ctx_count = lax.axis_size("ctx")
    device_index = lax.axis_index("ctx")
    core = device_index % 2
    exchange = functools.partial(
        lax.all_to_all,
        axis_name="ctx",
        split_axis=0,
        concat_axis=0,
        tiled=True,
        axis_index_groups=[list(range(parity, ctx_count, 2)) for parity in range(2)],
    )
    shape = jax.ShapeDtypeStruct
    (packed,) = call(
        pack_kernel,
        [shape((heads, rows, 3 * DH), jnp.bfloat16)],
        [VMEM] * 3,
        0,
        8,
        queries,
        keys,
        values,
    )
    own = exchange(packed)
    other = swap(own, 1)
    weights_own = (up_proj, expert_in[0], down_proj, expert_out[0])
    weights_other = tuple(swap(array, 1) for array in weights_own)
    weights = tuple(w for pair in zip(weights_own, weights_other) for w in pair)
    (out,) = call(
        attention_kernel,
        [shape((heads, rows + 16, DH), jnp.bfloat16)],
        [SMEM] + [VMEM] * 3,
        10**9,
        12,
        core.reshape(1),
        own,
        other,
        expert_ids.reshape(1, rows),
    )
    back = exchange(out)
    mixed, normed = call(
        project_kernel,
        [shape((rows, width), jnp.float32), shape((rows, width), jnp.bfloat16)],
        [VMEM] * 4,
        2 * out_proj.size * rows,
        12,
        back,
        out_proj,
        resid,
        norm_gain.reshape(1, width),
    )
    router_rows = router.astype(jnp.float32).T
    router_rows = jnp.where(core == 0, router_rows, router_rows[::-1])
    units = sum(w.size for w in weights[:4]) // width

    far_first = [4 * at for at in range(ctx_count // 4 - 1, 0, -1)]
    near = {0: normed}
    for offset in far_first:
        near[offset] = swap(normed, offset)
    across = {offset: swap(near[offset], 2) for offset in [0] + far_first}
    total = mixed
    for offset in far_first + [0]:
        places = [core] + [(device_index ^ mask) // 2 for mask in (offset, offset | 2)]
        part, part_across = call(
            mixture_kernel,
            [shape((rows, width), jnp.bfloat16)] * 2,
            [SMEM] + [VMEM] * 12,
            8 * rows * width * units,
            16,
            jnp.stack(places),
            near[offset],
            across[offset],
            back,
            router_rows,
            *weights,
        )
        summed = part.astype(jnp.float32) + swap(part_across, 2).astype(jnp.float32)
        if offset:
            summed = swap(summed.astype(jnp.bfloat16), offset).astype(jnp.float32)
        total = total + summed
    return total.astype(jnp.bfloat16)


def solution(mesh):
    ctx_count = mesh.shape["ctx"]

    def by_pairs(args):
        queries, router = args[0], args[8]
        return (
            router.shape[1] == 2
            and ctx_count == 2 * SPLIT
            and queries.shape[1] == ctx_count // 2 * DH
            and ctx_count % 4 == 0
            and ctx_count & (ctx_count - 1) == 0
        )

    def chosen(*args):
        if not by_pairs(args):
            return body(*args)
        return body_by_pairs(*args)

    placed = (
        P(("groups", "ctx"), None),
        P(("groups", "ctx"), None),
        P(("groups", "ctx"), None),
        P(("groups", "ctx"), None),
        P(),
        P(),
        P(None, "ctx"),
        P(None, "ctx"),
        P(),
        P(("groups", "ctx"), None),
        P("ctx", None, None),
        P("ctx", None, None),
    )
    return jax.shard_map(
        chosen, mesh=mesh, in_specs=placed, out_specs=P(("groups", "ctx"), None), check_vma=False
    )
```

profile of v0, /device:TPU:1, one launch (start us, length us, event | category | flops | bytes accessed | tf_op | source)
XLA Modules:
  0.0 196.8 jit_solution(5950203974990405055)
XLA Ops:
  0.0 1.1 copy-done.8
  1.1 0.9 copy-done.9
  4.1 6.4 %all-to-all-start = ((bf16[8,128,384]{2,1,0:T(8,128)(2,1)}), bf16[8,128,384]{2,1,0:T(8,128)(2,1)}, u32[]{:S(2)}, u32[]{:S(2)}) async-start(bf16[8,128,384]{2,1,0:T(8,128)(2,1)} %copy-done.5), calls=%async_computation | async-start | bytes 1572864 | tf_op jit(solution)/shard_map/all_to_all | solution.py:357
  10.4 1.0 collective-permute-start.4
  11.4 18.2 %all-to-all-done.own_ref = bf16[8,128,384]{2,1,0:T(8,128)(2,1)} async-done(((bf16[8,128,384]{2,1,0:T(8,128)(2,1)}), bf16[8,128,384]{2,1,0:T(8,128)(2,1)}, u32[]{:S(2)}, u32[]{:S(2)}) %all-to-all-start) | async-done | bytes 786464 | tf_op jit(solution)/shard_map/all_to_all | solution.py:357
  29.6 2.0 %collective-permute-start = (bf16[8,128,384]{2,1,0:T(8,128)(2,1)}, bf16[8,128,384]{2,1,0:T(8,128)(2,1)}, u32[]{:S(2)}, u32[]{:S(2)}) collective-permute-start(bf16[8,128,384]{2,1,0:T(8,128)(2,1)} %all-to-all-done.own_ref), channel_id=1, source_target_pairs={{0,1},{1,0},{2,3},{3,2},{4,5},{5,4},{6,7},{7,6},{8,9},{9,8},{10,11... | collective-permute-start | bytes 2359304 | tf_op jit(solution)/shard_map/ppermute | solution.py:180
  32.2 1.7 collective-permute-done.other_ref
  33.9 5.4 %shard_map.119 = bf16[8,144,128]{2,1,0:T(8,128)(2,1)S(1)} custom-call(s32[1]{0:T(128)} %bitcast.core_ref, bf16[8,128,384]{2,1,0:T(8,128)(2,1)} %all-to-all-done.own_ref, bf16[8,128,384]{2,1,0:T(8,128)(2,1)} %collective-permute-done.other_ref, s32[1,128]{1,0:T(1,128)S(1)} %bitcast.28), custom_call_target="tpu_custom_call" | custom-call | flops 1000000000 | bytes 1573380 | tf_op jit(solution)/shard_map/pallas_call | solution.py:188
  40.1 3.4 %all-to-all-start.1 = ((bf16[8,144,128]{2,1,0:T(8,128)(2,1)}), bf16[8,144,128]{2,1,0:T(8,128)(2,1)S(1)}, u32[]{:S(2)}, u32[]{:S(2)}) async-start(bf16[8,144,128]{2,1,0:T(8,128)(2,1)} %copy-done.7), calls=%async_computation.1 | async-start | bytes 589824 | tf_op jit(solution)/shard_map/all_to_all | solution.py:373
  44.4 7.3 %all-to-all-done.1.back_ref = bf16[8,144,128]{2,1,0:T(8,128)(2,1)S(1)} async-done(((bf16[8,144,128]{2,1,0:T(8,128)(2,1)}), bf16[8,144,128]{2,1,0:T(8,128)(2,1)S(1)}, u32[]{:S(2)}, u32[]{:S(2)}) %all-to-all-start.1) | async-done | bytes 294944 | tf_op jit(solution)/shard_map/all_to_all | solution.py:373
  51.7 2.2 %copy-done.4 = bf16[1024,2048]{1,0:T(8,128)(2,1)S(1)} copy-done((bf16[1024,2048]{1,0:T(8,128)(2,1)S(1)}, bf16[1024,2048]{1,0:T(8,128)(2,1)}, u32[]{:S(2)}) %copy-start.4) | copy-done | bytes 4194328
  53.9 1.0 copy-done.6
  55.8 2.2 %collective-permute-start.1 = (bf16[128,2048]{1,0:T(8,128)(2,1)S(1)}, bf16[128,2048]{1,0:T(8,128)(2,1)S(1)}, u32[]{:S(2)}, u32[]{:S(2)}) collective-permute-start(bf16[128,2048]{1,0:T(8,128)(2,1)S(1)} %get-tuple-element.16.first_ref), channel_id=1, source_target_pairs={{0,12},{1,13},{2,14},{3,15},{4,8},{5,9},{6,10},{7,11},{8,4},{9,5},... | collective-permute-start | bytes 1572872 | tf_op jit(solution)/shard_map/ppermute | solution.py:180
  58.1 1.9 collective-permute-start.17
  60.8 8.3 %collective-permute-done.1.first_ref = bf16[128,2048]{1,0:T(8,128)(2,1)S(1)} collective-permute-done((bf16[128,2048]{1,0:T(8,128)(2,1)S(1)}, bf16[128,2048]{1,0:T(8,128)(2,1)S(1)}, u32[]{:S(2)}, u32[]{:S(2)}) %collective-permute-start.1) | collective-permute-done | bytes 524320 | tf_op jit(solution)/shard_map/ppermute | solution.py:180
  69.0 1.5 collective-permute-start.2
  70.7 31.9 %collective-permute-done.9.first_ref = bf16[128,2048]{1,0:T(8,128)(2,1)S(1)} collective-permute-done((bf16[128,2048]{1,0:T(8,128)(2,1)S(1)}, bf16[128,2048]{1,0:T(8,128)(2,1)S(1)}, u32[]{:S(2)}, u32[]{:S(2)}) %collective-permute-start.9) | collective-permute-done | bytes 524320 | tf_op jit(solution)/shard_map/ppermute | solution.py:180
  102.7 6.8 %shard_map.124 = (bf16[128,2048]{1,0:T(8,128)(2,1)S(1)}, bf16[128,2048]{1,0:T(8,128)(2,1)S(1)}) custom-call(s32[3]{0:T(128)S(1)} %pad_add_fusion.3.at_ref, bf16[128,2048]{1,0:T(8,128)(2,1)S(1)} %get-tuple-element.16.first_ref, bf16[128,2048]{1,0:T(8,128)(2,1)S(1)} %collective-permute-done.17.second_ref, bf16[8,144,128]{2,1,0:T(8,128)(2,1)S(1)} %all-to-all-done.1.back_ref, ...), custom_call_target="tpu_custom_call" | custom-call | flops 3221225472 | bytes 13942796 | tf_op jit(solution)/shard_map/pallas_call | solution.py:188
  109.5 1.5 collective-permute-start.18
  111.1 6.8 %shard_map.121 = (bf16[128,2048]{1,0:T(8,128)(2,1)S(1)}, bf16[128,2048]{1,0:T(8,128)(2,1)S(1)}) custom-call(s32[3]{0:T(128)S(1)} %pad_add_fusion.at_ref, bf16[128,2048]{1,0:T(8,128)(2,1)S(1)} %collective-permute-done.1.first_ref, bf16[128,2048]{1,0:T(8,128)(2,1)S(1)} %collective-permute-done.2.second_ref, bf16[8,144,128]{2,1,0:T(8,128)(2,1)S(1)} %all-to-all-done.1.back_ref, ...), custom_call_target="tpu_custom_call" | custom-call | flops 3221225472 | bytes 13942796 | tf_op jit(solution)/shard_map/pallas_call | solution.py:188
  117.8 1.4 collective-permute-start.7
  119.3 6.8 %shard_map.122 = (bf16[128,2048]{1,0:T(8,128)(2,1)S(1)}, bf16[128,2048]{1,0:T(8,128)(2,1)S(1)}) custom-call(s32[3]{0:T(128)S(1)} %pad_add_fusion.1.at_ref, bf16[128,2048]{1,0:T(8,128)(2,1)S(1)} %collective-permute-done.9.first_ref, bf16[128,2048]{1,0:T(8,128)(2,1)S(1)} %collective-permute-done.10.second_ref, ...), custom_call_target="tpu_custom_call" | custom-call | flops 3221225472 | bytes 13942796 | tf_op jit(solution)/shard_map/pallas_call | solution.py:188
  126.2 10.6 %collective-permute-done.14.second_ref = bf16[128,2048]{1,0:T(8,128)(2,1)S(1)} collective-permute-done((bf16[128,2048]{1,0:T(8,128)(2,1)S(1)}, bf16[128,2048]{1,0:T(8,128)(2,1)S(1)}, u32[]{:S(2)}, u32[]{:S(2)}) %collective-permute-start.14) | collective-permute-done | bytes 524320 | tf_op jit(solution)/shard_map/ppermute | solution.py:180
  136.8 7.0 %shard_map.123 = (bf16[128,2048]{1,0:T(8,128)(2,1)S(1)}, bf16[128,2048]{1,0:T(8,128)(2,1)S(1)}) custom-call(s32[3]{0:T(128)S(1)} %pad_add_fusion.2.at_ref, bf16[128,2048]{1,0:T(8,128)(2,1)S(1)} %collective-permute-done.13.first_ref, bf16[128,2048]{1,0:T(8,128)(2,1)S(1)} %collective-permute-done.14.second_ref, ...), custom_call_target="tpu_custom_call" | custom-call | flops 3221225472 | bytes 13942796 | tf_op jit(solution)/shard_map/pallas_call | solution.py:188
  143.9 4.2 %collective-permute-done.7 = bf16[128,2048]{1,0:T(8,128)(2,1)S(1)} collective-permute-done((bf16[128,2048]{1,0:T(8,128)(2,1)S(1)}, bf16[128,2048]{1,0:T(8,128)(2,1)S(1)}, u32[]{:S(2)}, u32[]{:S(2)}) %collective-permute-start.7) | collective-permute-done | bytes 524320 | tf_op jit(solution)/shard_map/ppermute | solution.py:180
  148.2 2.9 %collective-permute-start.8 = (bf16[128,2048]{1,0:T(8,128)(2,1)S(1)}, bf16[128,2048]{1,0:T(8,128)(2,1)S(1)}, u32[]{:S(2)}, u32[]{:S(2)}) collective-permute-start(bf16[128,2048]{1,0:T(8,128)(2,1)S(1)} %add_convert_fusion.3), channel_id=1, source_target_pairs={{0,12},{1,13},{2,14},{3,15},{4,8},{5,9},{6,10},{7,11},{8,4},{9,5},... | collective-permute-start | bytes 1572872 | tf_op jit(solution)/shard_map/ppermute | solution.py:180
  151.1 8.2 %collective-permute-done.11 = bf16[128,2048]{1,0:T(8,128)(2,1)S(1)} collective-permute-done((bf16[128,2048]{1,0:T(8,128)(2,1)S(1)}, bf16[128,2048]{1,0:T(8,128)(2,1)S(1)}, u32[]{:S(2)}, u32[]{:S(2)}) %collective-permute-start.11) | collective-permute-done | bytes 524320 | tf_op jit(solution)/shard_map/ppermute | solution.py:180
  159.4 1.6 collective-permute-start.12
  161.0 9.5 %collective-permute-done.15 = bf16[128,2048]{1,0:T(8,128)(2,1)S(1)} collective-permute-done((bf16[128,2048]{1,0:T(8,128)(2,1)S(1)}, bf16[128,2048]{1,0:T(8,128)(2,1)S(1)}, u32[]{:S(2)}, u32[]{:S(2)}) %collective-permute-start.15) | collective-permute-done | bytes 524320 | tf_op jit(solution)/shard_map/ppermute | solution.py:180
  170.6 1.1 collective-permute-start.16
  171.7 23.7 %collective-permute-done.12 = bf16[128,2048]{1,0:T(8,128)(2,1)S(1)} collective-permute-done((bf16[128,2048]{1,0:T(8,128)(2,1)S(1)}, bf16[128,2048]{1,0:T(8,128)(2,1)S(1)}, u32[]{:S(2)}, u32[]{:S(2)}) %collective-permute-start.12) | collective-permute-done | bytes 524320 | tf_op jit(solution)/shard_map/ppermute | solution.py:180
  195.5 1.3 add_convert_fusion
  (56 shorter events, 6.5 us)
Async XLA Ops:
  0.0 10.4 %copy-start = (bf16[1,2048,512]{2,1,0:T(8,128)(2,1)S(1)}, bf16[1,2048,512]{2,1,0:T(8,128)(2,1)}, u32[]{:S(2)}) copy-start(bf16[1,2048,512]{2,1,0:T(8,128)(2,1)} %param.22) | copy-start | bytes 6291460
  0.0 31.7 %copy-start.2 = (bf16[2048,256]{1,0:T(8,128)(2,1)S(1)}, bf16[2048,256]{1,0:T(8,128)(2,1)}, u32[]{:S(2)}) copy-start(bf16[2048,256]{1,0:T(8,128)(2,1)} %up_a.7) | copy-start | bytes 3145732
  0.0 1.1 copy-start.8
  1.1 0.9 copy-start.9
  3.0 30.9 %copy-start.12 = (s32[128,1]{0,1:T(1,128)S(1)}, s32[128,1]{0,1:T(1,128)}, u32[]{:S(2)}) copy-start(s32[128,1]{0,1:T(1,128)} %param.21) | copy-start | bytes 1540
  4.1 25.6 %all-to-all-start = ((bf16[8,128,384]{2,1,0:T(8,128)(2,1)}), bf16[8,128,384]{2,1,0:T(8,128)(2,1)}, u32[]{:S(2)}, u32[]{:S(2)}) async-start(bf16[8,128,384]{2,1,0:T(8,128)(2,1)} %copy-done.5), calls=%async_computation | async-start | bytes 1572864 | tf_op jit(solution)/shard_map/all_to_all | solution.py:357
  10.4 49.6 %collective-permute-start.4 = (bf16[2048,512]{1,0:T(8,128)(2,1)S(1)}, bf16[2048,512]{1,0:T(8,128)(2,1)}, u32[]{:S(2)}, u32[]{:S(2)}) collective-permute-start(bf16[2048,512]{1,0:T(8,128)(2,1)S(1)} %bitcast.17), channel_id=1, source_target_pairs={{0,1},{1,0},{2,3},{3,2},{4,5},{5,4},{6,7},{7,6},{8,9},{9,8},{10,11... | collective-permute-start | bytes 6291464 | tf_op jit(solution)/shard_map/ppermute | solution.py:180
  29.6 4.3 %collective-permute-start = (bf16[8,128,384]{2,1,0:T(8,128)(2,1)}, bf16[8,128,384]{2,1,0:T(8,128)(2,1)}, u32[]{:S(2)}, u32[]{:S(2)}) collective-permute-start(bf16[8,128,384]{2,1,0:T(8,128)(2,1)} %all-to-all-done.own_ref), channel_id=1, source_target_pairs={{0,1},{1,0},{2,3},{3,2},{4,5},{5,4},{6,7},{7,6},{8,9},{9,8},{10,11... | collective-permute-start | bytes 2359304 | tf_op jit(solution)/shard_map/ppermute | solution.py:180
  31.7 71.0 %collective-permute-start.6 = (bf16[512,2048]{1,0:T(8,128)(2,1)}, bf16[512,2048]{1,0:T(8,128)(2,1)}, u32[]{:S(2)}, u32[]{:S(2)}) collective-permute-start(bf16[512,2048]{1,0:T(8,128)(2,1)} %bitcast.22), channel_id=1, source_target_pairs={{0,1},{1,0},{2,3},{3,2},{4,5},{5,4},{6,7},{7,6},{8,9},{9,8},{10,11... | collective-permute-start | bytes 6291464 | tf_op jit(solution)/shard_map/ppermute | solution.py:180
  31.7 26.4 %collective-permute-start.3 = (bf16[2048,256]{1,0:T(8,128)(2,1)S(1)}, bf16[2048,256]{1,0:T(8,128)(2,1)}, u32[]{:S(2)}, u32[]{:S(2)}) collective-permute-start(bf16[2048,256]{1,0:T(8,128)(2,1)S(1)} %copy-done.2), channel_id=1, source_target_pairs={{0,1},{1,0},{2,3},{3,2},{4,5},{5,4},{6,7},{7,6},{8,9},{9,8},{10,11... | collective-permute-start | bytes 3145736 | tf_op jit(solution)/shard_map/ppermute | solution.py:180
  32.2 25.9 %collective-permute-start.5 = (bf16[2048,256]{1,0:T(8,128)(2,1)}, bf16[2048,256]{1,0:T(8,128)(2,1)}, u32[]{:S(2)}, u32[]{:S(2)}) collective-permute-start(bf16[2048,256]{1,0:T(8,128)(2,1)} %down_a.7), channel_id=1, source_target_pairs={{0,1},{1,0},{2,3},{3,2},{4,5},{5,4},{6,7},{7,6},{8,9},{9,8},{10,11... | collective-permute-start | bytes 3145736 | tf_op jit(solution)/shard_map/ppermute | solution.py:180
  33.9 9.6 %copy-start.13 = (bf16[2048,2]{0,1:T(2,128)(2,1)S(1)}, bf16[2048,2]{0,1:T(2,128)(2,1)}, u32[]{:S(2)}) copy-start(bf16[2048,2]{0,1:T(2,128)(2,1)} %param.20) | copy-start | bytes 24580
  33.9 17.8 %copy-start.11 = (f32[2048]{0:T(1024)S(1)}, f32[2048]{0:T(1024)}, u32[]{:S(2)}) copy-start(f32[2048]{0:T(1024)} %param.17) | copy-start | bytes 24580
  40.1 11.6 %all-to-all-start.1 = ((bf16[8,144,128]{2,1,0:T(8,128)(2,1)}), bf16[8,144,128]{2,1,0:T(8,128)(2,1)S(1)}, u32[]{:S(2)}, u32[]{:S(2)}) async-start(bf16[8,144,128]{2,1,0:T(8,128)(2,1)} %copy-done.7), calls=%async_computation.1 | async-start | bytes 589824 | tf_op jit(solution)/shard_map/all_to_all | solution.py:373
  51.7 2.2 %copy-start.4 = (bf16[1024,2048]{1,0:T(8,128)(2,1)S(1)}, bf16[1024,2048]{1,0:T(8,128)(2,1)}, u32[]{:S(2)}) copy-start(bf16[1024,2048]{1,0:T(8,128)(2,1)} %weight_ref.1) | copy-start | bytes 12582916
  53.9 1.0 copy-start.6
  54.9 47.7 %copy-start.1 = (bf16[1,512,2048]{2,1,0:T(8,128)(2,1)S(1)}, bf16[1,512,2048]{2,1,0:T(8,128)(2,1)}, u32[]{:S(2)}) copy-start(bf16[1,512,2048]{2,1,0:T(8,128)(2,1)} %param.23) | copy-start | bytes 6291460
  54.9 47.8 %copy-start.3 = (bf16[2048,256]{1,0:T(8,128)(2,1)S(1)}, bf16[2048,256]{1,0:T(8,128)(2,1)}, u32[]{:S(2)}) copy-start(bf16[2048,256]{1,0:T(8,128)(2,1)} %down_a.7) | copy-start | bytes 3145732
  55.8 13.2 %collective-permute-start.1 = (bf16[128,2048]{1,0:T(8,128)(2,1)S(1)}, bf16[128,2048]{1,0:T(8,128)(2,1)S(1)}, u32[]{:S(2)}, u32[]{:S(2)}) collective-permute-start(bf16[128,2048]{1,0:T(8,128)(2,1)S(1)} %get-tuple-element.16.first_ref), channel_id=1, source_target_pairs={{0,12},{1,13},{2,14},{3,15},{4,8},{5,9},{6,10},{7,11},{8,4},{9,5},... | collective-permute-start | bytes 1572872 | tf_op jit(solution)/shard_map/ppermute | solution.py:180
  58.1 44.6 %collective-permute-start.9 = (bf16[128,2048]{1,0:T(8,128)(2,1)S(1)}, bf16[128,2048]{1,0:T(8,128)(2,1)S(1)}, u32[]{:S(2)}, u32[]{:S(2)}) collective-permute-start(bf16[128,2048]{1,0:T(8,128)(2,1)S(1)} %get-tuple-element.16.first_ref), channel_id=1, source_target_pairs={{0,8},{1,9},{2,10},{3,11},{4,12},{5,13},{6,14},{7,15},{8,0},{9,1},... | collective-permute-start | bytes 1572872 | tf_op jit(solution)/shard_map/ppermute | solution.py:180
  58.1 44.5 %collective-permute-start.17 = (bf16[128,2048]{1,0:T(8,128)(2,1)S(1)}, bf16[128,2048]{1,0:T(8,128)(2,1)S(1)}, u32[]{:S(2)}, u32[]{:S(2)}) collective-permute-start(bf16[128,2048]{1,0:T(8,128)(2,1)S(1)} %get-tuple-element.16.first_ref), channel_id=1, source_target_pairs={{0,2},{1,3},{2,0},{3,1},{4,6},{5,7},{6,4},{7,5},{8,10},{9,11},{10,... | collective-permute-start | bytes 1572872 | tf_op jit(solution)/shard_map/ppermute | solution.py:180
  60.0 51.0 %collective-permute-start.13 = (bf16[128,2048]{1,0:T(8,128)(2,1)S(1)}, bf16[128,2048]{1,0:T(8,128)(2,1)S(1)}, u32[]{:S(2)}, u32[]{:S(2)}) collective-permute-start(bf16[128,2048]{1,0:T(8,128)(2,1)S(1)} %get-tuple-element.16.first_ref), channel_id=1, source_target_pairs={{0,4},{1,5},{2,6},{3,7},{4,0},{5,1},{6,2},{7,3},{8,12},{9,13},{10,... | collective-permute-start | bytes 1572872 | tf_op jit(solution)/shard_map/ppermute | solution.py:180
  69.0 42.0 %collective-permute-start.2 = (bf16[128,2048]{1,0:T(8,128)(2,1)S(1)}, bf16[128,2048]{1,0:T(8,128)(2,1)S(1)}, u32[]{:S(2)}, u32[]{:S(2)}) collective-permute-start(bf16[128,2048]{1,0:T(8,128)(2,1)S(1)} %collective-permute-done.1.first_ref), channel_id=1, source_target_pairs={{0,2},{1,3},{2,0},{3,1},{4,6},{5,7},{6,4},{7,5},{8,10},{9,11},{10,... | collective-permute-start | bytes 1572872 | tf_op jit(solution)/shard_map/ppermute | solution.py:180
  102.6 16.6 %collective-permute-start.10 = (bf16[128,2048]{1,0:T(8,128)(2,1)S(1)}, bf16[128,2048]{1,0:T(8,128)(2,1)S(1)}, u32[]{:S(2)}, u32[]{:S(2)}) collective-permute-start(bf16[128,2048]{1,0:T(8,128)(2,1)S(1)} %collective-permute-done.9.first_ref), channel_id=1, source_target_pairs={{0,2},{1,3},{2,0},{3,1},{4,6},{5,7},{6,4},{7,5},{8,10},{9,11},{10,... | collective-permute-start | bytes 1572872 | tf_op jit(solution)/shard_map/ppermute | solution.py:180
  109.5 62.3 %collective-permute-start.18 = (bf16[128,2048]{1,0:T(8,128)(2,1)S(1)}, bf16[128,2048]{1,0:T(8,128)(2,1)S(1)}, u32[]{:S(2)}, u32[]{:S(2)}) collective-permute-start(bf16[128,2048]{1,0:T(8,128)(2,1)S(1)} %get-tuple-element.24), channel_id=1, source_target_pairs={{0,2},{1,3},{2,0},{3,1},{4,6},{5,7},{6,4},{7,5},{8,10},{9,11},{10,... | collective-permute-start | bytes 1572872 | tf_op jit(solution)/shard_map/ppermute | solution.py:180
  111.0 25.8 %collective-permute-start.14 = (bf16[128,2048]{1,0:T(8,128)(2,1)S(1)}, bf16[128,2048]{1,0:T(8,128)(2,1)S(1)}, u32[]{:S(2)}, u32[]{:S(2)}) collective-permute-start(bf16[128,2048]{1,0:T(8,128)(2,1)S(1)} %collective-permute-done.13.first_ref), channel_id=1, source_target_pairs={{0,2},{1,3},{2,0},{3,1},{4,6},{5,7},{6,4},{7,5},{8,10},{9,11},{10,... | collective-permute-start | bytes 1572872 | tf_op jit(solution)/shard_map/ppermute | solution.py:180
  117.8 30.2 %collective-permute-start.7 = (bf16[128,2048]{1,0:T(8,128)(2,1)S(1)}, bf16[128,2048]{1,0:T(8,128)(2,1)S(1)}, u32[]{:S(2)}, u32[]{:S(2)}) collective-permute-start(bf16[128,2048]{1,0:T(8,128)(2,1)S(1)} %get-tuple-element.18), channel_id=1, source_target_pairs={{0,2},{1,3},{2,0},{3,1},{4,6},{5,7},{6,4},{7,5},{8,10},{9,11},{10,... | collective-permute-start | bytes 1572872 | tf_op jit(solution)/shard_map/ppermute | solution.py:180
  126.1 33.2 %collective-permute-start.11 = (bf16[128,2048]{1,0:T(8,128)(2,1)S(1)}, bf16[128,2048]{1,0:T(8,128)(2,1)S(1)}, u32[]{:S(2)}, u32[]{:S(2)}) collective-permute-start(bf16[128,2048]{1,0:T(8,128)(2,1)S(1)} %get-tuple-element.20), channel_id=1, source_target_pairs={{0,2},{1,3},{2,0},{3,1},{4,6},{5,7},{6,4},{7,5},{8,10},{9,11},{10,... | collective-permute-start | bytes 1572872 | tf_op jit(solution)/shard_map/ppermute | solution.py:180
  143.8 26.7 %collective-permute-start.15 = (bf16[128,2048]{1,0:T(8,128)(2,1)S(1)}, bf16[128,2048]{1,0:T(8,128)(2,1)S(1)}, u32[]{:S(2)}, u32[]{:S(2)}) collective-permute-start(bf16[128,2048]{1,0:T(8,128)(2,1)S(1)} %get-tuple-element.22), channel_id=1, source_target_pairs={{0,2},{1,3},{2,0},{3,1},{4,6},{5,7},{6,4},{7,5},{8,10},{9,11},{10,... | collective-permute-start | bytes 1572872 | tf_op jit(solution)/shard_map/ppermute | solution.py:180
  148.2 23.6 %collective-permute-start.8 = (bf16[128,2048]{1,0:T(8,128)(2,1)S(1)}, bf16[128,2048]{1,0:T(8,128)(2,1)S(1)}, u32[]{:S(2)}, u32[]{:S(2)}) collective-permute-start(bf16[128,2048]{1,0:T(8,128)(2,1)S(1)} %add_convert_fusion.3), channel_id=1, source_target_pairs={{0,12},{1,13},{2,14},{3,15},{4,8},{5,9},{6,10},{7,11},{8,4},{9,5},... | collective-permute-start | bytes 1572872 | tf_op jit(solution)/shard_map/ppermute | solution.py:180
  159.4 36.1 %collective-permute-start.12 = (bf16[128,2048]{1,0:T(8,128)(2,1)S(1)}, bf16[128,2048]{1,0:T(8,128)(2,1)S(1)}, u32[]{:S(2)}, u32[]{:S(2)}) collective-permute-start(bf16[128,2048]{1,0:T(8,128)(2,1)S(1)} %add_convert_fusion.2), channel_id=1, source_target_pairs={{0,8},{1,9},{2,10},{3,11},{4,12},{5,13},{6,14},{7,15},{8,0},{9,1},... | collective-permute-start | bytes 1572872 | tf_op jit(solution)/shard_map/ppermute | solution.py:180
  170.6 24.8 %collective-permute-start.16 = (bf16[128,2048]{1,0:T(8,128)(2,1)S(1)}, bf16[128,2048]{1,0:T(8,128)(2,1)S(1)}, u32[]{:S(2)}, u32[]{:S(2)}) collective-permute-start(bf16[128,2048]{1,0:T(8,128)(2,1)S(1)} %add_convert_fusion.1), channel_id=1, source_target_pairs={{0,4},{1,5},{2,6},{3,7},{4,0},{5,1},{6,2},{7,3},{8,12},{9,13},{10,... | collective-permute-start | bytes 1572872 | tf_op jit(solution)/shard_map/ppermute | solution.py:180
  (3 other events, 2.6 us)
where the time goes:
time: 199 us; the launch traced here: 197 us
  waiting for transfers between devices  124 us (62%)
  Pallas kernels  33.8 us (17%)
  starting transfers between devices  28.6 us (14%)
  local copies, waits for them, and re-layouts  8.44 us (4%)
    ppermute x19, waiting for transfers between devices, swap(): lax.ppermute(array, 'ctx', [(i, i ^ mask) for i in range(lax.axis_size('c...  98.2 us
    pallas_call x7, Pallas kernels, call(): pl.pallas_call(kernel, out_shape=outs, in_specs=specs, out_specs=[VMEM] *...  33.8 us
    ppermute x19, starting transfers between devices, swap(): lax.ppermute(array, 'ctx', [(i, i ^ mask) for i in range(lax.axis_size('c...  18.8 us
    all_to_all x1, waiting for transfers between devices, body_by_pairs(): own = exchange(packed)  18.2 us
    unnamed x28, local copies, waits for them, and re-layouts  7.85 us
    all_to_all x1, waiting for transfers between devices, body_by_pairs(): back = exchange(out)  7.31 us
    all_to_all x1, starting transfers between devices, body_by_pairs(): own = exchange(packed)  6.37 us
  transfers between devices with their start and end apart: 21, of which 10 were waited for; matrix products, arithmetic and copies ran while one was open for 1% of the time, Pallas kernels for 17%

commit v1 on v0

--- a/solution.py
+++ b/solution.py
@@ -184,12 +184,16 @@
 SMEM = pl.BlockSpec(memory_space=pltpu.SMEM)
 
 
-def call(kernel, outs, specs, flops, mib, *operands):
+HBM = pl.BlockSpec(memory_space=pltpu.HBM)
+
+
+def call(kernel, outs, specs, flops, mib, *operands, copies=0, scratch=()):
     return pl.pallas_call(
         kernel,
         out_shape=outs,
         in_specs=specs,
         out_specs=[VMEM] * len(outs),
+        scratch_shapes=[*scratch] + ([pltpu.SemaphoreType.DMA((copies,))] if copies else []),
         compiler_params=pltpu.CompilerParams(vmem_limit_bytes=mib * 2**20),
         cost_estimate=pl.CostEstimate(
             flops=flops,
@@ -199,15 +203,38 @@
     )(*operands)
 
 
-def pack_kernel(query_ref, key_ref, value_ref, out_ref):
-    for head in range(out_ref.shape[0]):
-        columns = slice(head * DH, (head + 1) * DH)
-        for at, ref in enumerate((query_ref, key_ref, value_ref)):
-            out_ref[head, :, at * DH : (at + 1) * DH] = ref[:, columns]
-
-
-def attention_kernel(core_ref, own_ref, other_ref, ids_ref, out_ref):
-    core = core_ref[0]
+def copy_all(pairs, sems):
+    copies = [pltpu.make_async_copy(a, b, sems.at[at]) for at, (a, b) in enumerate(pairs)]
+    for copy in copies:
+        copy.start()
+    for copy in copies:
+        copy.wait()
+
+
+def load_kernel(*refs):
+    count = len(refs) // 2
+    copy_all(zip(refs[:count], refs[count : 2 * count]), refs[-1])
+
+
+def load(*arrays):
+    outs = [pltpu.VMEM(array.shape, array.dtype) for array in arrays]
+    count = len(arrays)
+    return call(load_kernel, outs, [HBM] * count, 0, 36, *arrays, copies=count)
+
+
+def pack_kernel(query_ref, key_ref, value_ref, out_ref, sems):
+    copy_all(
+        [
+            (ref.at[:, pl.ds(head * DH, DH)], out_ref.at[head, :, pl.ds(at * DH, DH)])
+            for at, ref in enumerate((query_ref, key_ref, value_ref))
+            for head in range(out_ref.shape[0])
+        ],
+        sems,
+    )
+
+
+def attention_kernel(index_ref, own_ref, other_ref, ids_ref, out_ref):
+    core = index_ref[0] & 1
     blocks, rows, _ = own_ref.shape
     row_at = lax.broadcasted_iota(jnp.int32, (rows, rows), 0)
     column_at = lax.broadcasted_iota(jnp.int32, (rows, rows), 1)
@@ -251,19 +278,33 @@
         out_ref[block, rows:, :] = id_rows
 
 
-def project_kernel(back_ref, weight_ref, resid_ref, gain_ref, mixed_ref, normed_ref):
+def project_kernel(back_ref, weight_ref, resid_ref, gain_ref, mixed_ref, normed_ref, held, resid, sems):
     rows = resid_ref.shape[0]
+    pieces = held.shape[0]
+    depth = held.shape[1]
+    copies = [
+        pltpu.make_async_copy(weight_ref.at[pl.ds(at * depth, depth), :], held.at[at], sems.at[at])
+        for at in range(pieces)
+    ]
+    copies.append(pltpu.make_async_copy(resid_ref, resid, sems.at[pieces]))
+    for copy in copies[-1:] + copies[:-1]:
+        copy.start()
     attn = jnp.concatenate([back_ref[head, :rows, :] for head in range(back_ref.shape[0])], axis=1)
-    mixed = resid_ref[...].astype(jnp.float32) + jnp.dot(
-        attn, weight_ref[...], preferred_element_type=jnp.float32
-    )
+    copies[-1].wait()
+    mixed = resid[...].astype(jnp.float32)
+    for at in range(pieces):
+        copies[at].wait()
+        mixed = mixed + jnp.dot(
+            attn[:, at * depth : (at + 1) * depth], held[at], preferred_element_type=jnp.float32
+        )
     mixed_ref[...] = mixed
     scale = lax.rsqrt(jnp.mean(mixed * mixed, axis=1, keepdims=True) + EPSILON)
     normed_ref[...] = (mixed * scale * gain_ref[...]).astype(jnp.bfloat16)
 
 
 def mixture_kernel(
-    at_ref,
+    offset,
+    index_ref,
     first_ref,
     second_ref,
     back_ref,
@@ -280,15 +321,17 @@
     second_out,
 ):
     rows, width = first_ref.shape
-    own = at_ref[0].astype(jnp.float32)
-
-    def is_own(shard):
-        ids = back_ref[shard, rows : rows + 16, :].astype(jnp.float32)[0:1, :]
-        return (jnp.transpose(jnp.broadcast_to(ids, (rows, rows)))[:, 0:1] == own).astype(jnp.float32)
+    own = (index_ref[0] & 1).astype(jnp.float32)
+
+    def expert(mask):
+        ids = back_ref[(index_ref[0] ^ mask) >> 1, rows : rows + 16, :].astype(jnp.float32)[0:1, :]
+        return jnp.transpose(jnp.broadcast_to(ids, (rows, rows)))[:, 0:1]
 
     normed = jnp.concatenate([first_ref[...], second_ref[...]], axis=0)
-    mine = jnp.concatenate([is_own(at_ref[1]), is_own(at_ref[2])], axis=0)
-    column = jnp.where(mine > 0, router_ref[0:1, :], router_ref[1:2, :])
+    chosen = jnp.concatenate([expert(offset), expert(offset | 2)], axis=0)
+    mine = chosen == own
+    router = router_ref[...].astype(jnp.float32)
+    column = jnp.where(chosen > 0, router[1:2, :], router[0:1, :])
     logits = jnp.sum(normed.astype(jnp.float32) * column, axis=1, keepdims=True)
     gate = jax.nn.sigmoid(logits)
 
@@ -297,8 +340,8 @@
 
     mlp_a = hidden(up_a).astype(jnp.bfloat16)
     mlp_b = hidden(up_b).astype(jnp.bfloat16)
-    exp_a = jnp.where(mine > 0, hidden(in_a), 0.0).astype(jnp.bfloat16)
-    exp_b = jnp.where(mine > 0, 0.0, hidden(in_b)).astype(jnp.bfloat16)
+    exp_a = jnp.where(mine, hidden(in_a), 0.0).astype(jnp.bfloat16)
+    exp_b = jnp.where(mine, 0.0, hidden(in_b)).astype(jnp.bfloat16)
     contract = (((1,), (1,)), ((), ()))
     step = min(width, 512)
     for begin in range(0, width, step):
@@ -334,7 +377,7 @@
     heads = queries.shape[1] // DH
     ctx_count = lax.axis_size("ctx")
     device_index = lax.axis_index("ctx")
-    core = device_index % 2
+    index = device_index.reshape(1)
     exchange = functools.partial(
         lax.all_to_all,
         axis_name="ctx",
@@ -347,17 +390,20 @@
     (packed,) = call(
         pack_kernel,
         [shape((heads, rows, 3 * DH), jnp.bfloat16)],
-        [VMEM] * 3,
+        [HBM] * 3,
         0,
-        8,
+        62,
         queries,
         keys,
         values,
+        copies=3 * heads,
     )
     own = exchange(packed)
     other = swap(own, 1)
     weights_own = (up_proj, expert_in[0], down_proj, expert_out[0])
-    weights_other = tuple(swap(array, 1) for array in weights_own)
+    weights_other = [swap(array, 1) for array in weights_own]
+    weights_own = load(*weights_own)
+    weights_other = load(*weights_other)
     weights = tuple(w for pair in zip(weights_own, weights_other) for w in pair)
     (out,) = call(
         attention_kernel,
@@ -365,52 +411,65 @@
         [SMEM] + [VMEM] * 3,
         10**9,
         12,
-        core.reshape(1),
+        index,
         own,
         other,
         expert_ids.reshape(1, rows),
     )
     back = exchange(out)
+    pieces = heads // 2
     mixed, normed = call(
         project_kernel,
-        [shape((rows, width), jnp.float32), shape((rows, width), jnp.bfloat16)],
-        [VMEM] * 4,
+        [pltpu.VMEM((rows, width), jnp.float32), shape((rows, width), jnp.bfloat16)],
+        [VMEM, HBM, HBM, VMEM],
         2 * out_proj.size * rows,
-        12,
+        58,
         back,
         out_proj,
         resid,
         norm_gain.reshape(1, width),
-    )
-    router_rows = router.astype(jnp.float32).T
-    router_rows = jnp.where(core == 0, router_rows, router_rows[::-1])
+        copies=pieces + 1,
+        scratch=[
+            pltpu.VMEM((pieces, out_proj.shape[0] // pieces, width), out_proj.dtype),
+            pltpu.VMEM(resid.shape, resid.dtype),
+        ],
+    )
     units = sum(w.size for w in weights[:4]) // width
 
-    far_first = [4 * at for at in range(ctx_count // 4 - 1, 0, -1)]
-    near = {0: normed}
-    for offset in far_first:
-        near[offset] = swap(normed, offset)
-    across = {offset: swap(near[offset], 2) for offset in [0] + far_first}
-    total = mixed
-    for offset in far_first + [0]:
-        places = [core] + [(device_index ^ mask) // 2 for mask in (offset, offset | 2)]
-        part, part_across = call(
-            mixture_kernel,
-            [shape((rows, width), jnp.bfloat16)] * 2,
+    def mix(offset, first, second):
+        return call(
+            functools.partial(mixture_kernel, offset),
+            [pltpu.VMEM((rows, width), jnp.bfloat16)] * 2,
             [SMEM] + [VMEM] * 12,
             8 * rows * width * units,
             16,
-            jnp.stack(places),
-            near[offset],
-            across[offset],
+            index,
+            first,
+            second,
             back,
-            router_rows,
+            router.T,
             *weights,
         )
-        summed = part.astype(jnp.float32) + swap(part_across, 2).astype(jnp.float32)
-        if offset:
-            summed = swap(summed.astype(jnp.bfloat16), offset).astype(jnp.float32)
-        total = total + summed
+
+    def plus(first, second):
+        return first.astype(jnp.float32) + second.astype(jnp.float32)
+
+    far = [4 * at for at in range(ctx_count // 4 - 1, 1, -1)]
+    gathered = {offset: swap(normed, offset) for offset in far}
+    across = swap(normed, 2)
+    beside = swap(normed, 4)
+    beside_across = swap(across, 4)
+    total = mixed
+    for offset in far:
+        first = gathered[offset]
+        part, part_across = mix(offset, first, swap(first, 2))
+        summed = plus(part, swap(part_across, 2)).astype(jnp.bfloat16)
+        total = total + swap(summed, offset).astype(jnp.float32)
+    part, part_across = mix(0, normed, across)
+    part_beside, part_both = mix(4, beside, beside_across)
+    summed = plus(part_across, swap(part_both, 4)).astype(jnp.bfloat16)
+    total = total + plus(part, swap(part_beside, 4))
+    total = total + swap(summed, 2).astype(jnp.float32)
     return total.astype(jnp.bfloat16)
 
 

time: 199 us -> 179 us (0.90)
  the two profiles are of different devices: /device:TPU:1 before, /device:TPU:0 now
where the time goes in v1:
time: 179 us; the launch traced here: 178 us
  waiting for transfers between devices  68.3 us (38%)
  blocking collectives  41.6 us (23%)
  starting transfers between devices  34.7 us (19%)
  Pallas kernels  31.9 us (18%)
    ppermute x19, waiting for transfers between devices, swap(): lax.ppermute(array, 'ctx', [(i, i ^ mask) for i in range(lax.axis_size('c...  68.3 us
    ppermute x19, starting transfers between devices, swap(): lax.ppermute(array, 'ctx', [(i, i ^ mask) for i in range(lax.axis_size('c...  34.7 us
    pallas_call x9, Pallas kernels, call(): pl.pallas_call(kernel, out_shape=outs, in_specs=specs, out_specs=[VMEM] *...  31.9 us
    all_to_all x1, blocking collectives, body_by_pairs(): own = exchange(packed)  27.5 us
    all_to_all x1, blocking collectives, body_by_pairs(): back = exchange(out)  14.1 us
  transfers between devices with their start and end apart: 19, of which 9 were waited for; matrix products, arithmetic and copies ran while one was open for 0% of the time, Pallas kernels for 17%

profile of v1, /device:TPU:0, one launch (start us, length us, event | category | flops | bytes accessed | tf_op | source)
XLA Modules:
  0.0 178.5 jit_solution(1233847938843303112)
XLA Ops:
  0.0 2.2 %shard_map.118 = bf16[8,128,384]{2,1,0:T(8,128)(2,1)} custom-call(bf16[128,1024]{1,0:T(8,128)(2,1)} %query_ref.1, bf16[128,1024]{1,0:T(8,128)(2,1)} %key_ref.1, bf16[128,1024]{1,0:T(8,128)(2,1)} %value_ref.1), custom_call_target="tpu_custom_call" | custom-call | bytes 786432 | tf_op jit(solution)/shard_map/pallas_call | solution.py:191
  2.2 27.5 %all_to_all.10.own_ref = bf16[8,128,384]{2,1,0:T(8,128)(2,1)S(1)} all-to-all(bf16[8,128,384]{2,1,0:T(8,128)(2,1)} %shard_map.118), channel_id=1, replica_groups={{0,2,4,6,8,10,12,14},{1,3,5,7,9,11,13,15},{16,18,20,22,24,26,28,30},{17..., dimensions={0} | all-to-all | bytes 1572864 | tf_op jit(solution)/shard_map/all_to_all | solution.py:401
  30.7 1.3 collective-permute-done.other_ref
  32.0 4.1 %shard_map.119 = bf16[8,144,128]{2,1,0:T(8,128)(2,1)S(1)} custom-call(s32[1]{0:T(128)} %bitcast.index_ref, bf16[8,128,384]{2,1,0:T(8,128)(2,1)S(1)} %all_to_all.10.own_ref, bf16[8,128,384]{2,1,0:T(8,128)(2,1)S(1)} %collective-permute-done.other_ref, s32[1,128]{1,0:T(1,128)S(1)} %bitcast.14), custom_call_target="tpu_custom_call" | custom-call | flops 1000000000 | bytes 1573380 | tf_op jit(solution)/shard_map/pallas_call | solution.py:191
  36.1 14.1 %all_to_all.11.back_ref = bf16[8,144,128]{2,1,0:T(8,128)(2,1)} all-to-all(bf16[8,144,128]{2,1,0:T(8,128)(2,1)S(1)} %shard_map.119), channel_id=1, replica_groups={{0,2,4,6,8,10,12,14},{1,3,5,7,9,11,13,15},{16,18,20,22,24,26,28,30},{17..., dimensions={0} | all-to-all | bytes 589824 | tf_op jit(solution)/shard_map/all_to_all | solution.py:419
  50.2 5.0 %shard_map.120 = (f32[128,2048]{1,0:T(8,128)S(1)}, bf16[128,2048]{1,0:T(8,128)(2,1)}) custom-call(bf16[8,144,128]{2,1,0:T(8,128)(2,1)} %all_to_all.11.back_ref, bf16[1024,2048]{1,0:T(8,128)(2,1)} %weight_ref.1, bf16[128,2048]{1,0:T(8,128)(2,1)} %resid_ref.1, f32[1,2048]{1,0:T(1,128)} %bitcast.15), custom_call_target="tpu_custom_call" | custom-call | flops 536870912 | bytes 5021696 | tf_op jit(solution)/shard_map/pallas_call | solution.py:191
  55.2 1.5 collective-permute-start.1
  56.8 0.7 collective-permute-start.9
  57.4 0.5 collective-permute-start.13
  57.9 14.2 %collective-permute-done.1.first_ref = bf16[128,2048]{1,0:T(8,128)(2,1)S(1)} collective-permute-done((bf16[128,2048]{1,0:T(8,128)(2,1)}, bf16[128,2048]{1,0:T(8,128)(2,1)S(1)}, u32[]{:S(2)}, u32[]{:S(2)}) %collective-permute-start.1) | collective-permute-done | bytes 524320 | tf_op jit(solution)/shard_map/ppermute | solution.py:180
  72.2 0.7 collective-permute-start.2
  72.9 1.6 shard_map.121
  74.5 3.0 %shard_map.122 = (bf16[2048,256]{1,0:T(8,128)(2,1)S(1)}, bf16[2048,512]{1,0:T(8,128)(2,1)S(1)}, bf16[2048,256]{1,0:T(8,128)(2,1)S(1)}, bf16[512,2048]{1,0:T(8,128)(2,1)S(1)}) custom-call(bf16[2048,256]{1,0:T(8,128)(2,1)} %collective-permute-done.3.refs_0_, bf16[2048,512]{1,0:T(8,128)(2,1)} %collective-permute-done.4.refs_1_, ...), custom_call_target="tpu_custom_call" | custom-call | bytes 6291456 | tf_op jit(solution)/shard_map/pallas_call | solution.py:191
  77.5 20.3 %collective-permute-start.14 = (bf16[128,2048]{1,0:T(8,128)(2,1)S(1)}, bf16[128,2048]{1,0:T(8,128)(2,1)S(1)}, u32[]{:S(2)}, u32[]{:S(2)}) collective-permute-start(bf16[128,2048]{1,0:T(8,128)(2,1)S(1)} %copy-done.3), channel_id=1, source_target_pairs={{0,4},{1,5},{2,6},{3,7},{4,0},{5,1},{6,2},{7,3},{8,12},{9,13},{10,... | collective-permute-start | bytes 1572872 | tf_op jit(solution)/shard_map/ppermute | solution.py:180
  97.8 3.7 %collective-permute-done.9.first_ref = bf16[128,2048]{1,0:T(8,128)(2,1)S(1)} collective-permute-done((bf16[128,2048]{1,0:T(8,128)(2,1)}, bf16[128,2048]{1,0:T(8,128)(2,1)S(1)}, u32[]{:S(2)}, u32[]{:S(2)}) %collective-permute-start.9) | collective-permute-done | bytes 524320 | tf_op jit(solution)/shard_map/ppermute | solution.py:180
  101.5 0.7 collective-permute-start.10
  102.3 3.9 %shard_map.125 = (bf16[128,2048]{1,0:T(8,128)(2,1)S(1)}, bf16[128,2048]{1,0:T(8,128)(2,1)S(1)}) custom-call(s32[1]{0:T(128)} %bitcast.index_ref, bf16[128,2048]{1,0:T(8,128)(2,1)S(1)} %copy-done.3, bf16[128,2048]{1,0:T(8,128)(2,1)S(1)} %collective-permute-done.13.second_ref, bf16[8,144,128]{2,1,0:T(8,128)(2,1)S(1)} %copy-done, bf16[2,2048]{1,0:T(2,128)(2,1)S(1)} %bitcast.10, ...), custom_call_target="tpu_custom_call" | custom-call | flops 3221225472 | bytes 13934596 | tf_op jit(solution)/shard_map/pallas_call | solution.py:191
  106.2 3.9 %shard_map.123 = (bf16[128,2048]{1,0:T(8,128)(2,1)S(1)}, bf16[128,2048]{1,0:T(8,128)(2,1)S(1)}) custom-call(s32[1]{0:T(128)} %bitcast.index_ref, bf16[128,2048]{1,0:T(8,128)(2,1)S(1)} %collective-permute-done.1.first_ref, bf16[128,2048]{1,0:T(8,128)(2,1)S(1)} %collective-permute-done.2.second_ref, bf16[8,144,128]{2,1,0:T(8,128)(2,1)S(1)} %copy-done, ...), custom_call_target="tpu_custom_call" | custom-call | flops 3221225472 | bytes 13934596 | tf_op jit(solution)/shard_map/pallas_call | solution.py:191
  110.2 1.3 collective-permute-start.7
  111.5 4.8 %collective-permute-done.10.second_ref = bf16[128,2048]{1,0:T(8,128)(2,1)S(1)} collective-permute-done((bf16[128,2048]{1,0:T(8,128)(2,1)S(1)}, bf16[128,2048]{1,0:T(8,128)(2,1)S(1)}, u32[]{:S(2)}, u32[]{:S(2)}) %collective-permute-start.10) | collective-permute-done | bytes 524320 | tf_op jit(solution)/shard_map/ppermute | solution.py:180
  116.3 3.9 %shard_map.124 = (bf16[128,2048]{1,0:T(8,128)(2,1)S(1)}, bf16[128,2048]{1,0:T(8,128)(2,1)S(1)}) custom-call(s32[1]{0:T(128)} %bitcast.index_ref, bf16[128,2048]{1,0:T(8,128)(2,1)S(1)} %collective-permute-done.9.first_ref, bf16[128,2048]{1,0:T(8,128)(2,1)S(1)} %collective-permute-done.10.second_ref, bf16[8,144,128]{2,1,0:T(8,128)(2,1)S(1)} %copy-done, ...), custom_call_target="tpu_custom_call" | custom-call | flops 3221225472 | bytes 13934596 | tf_op jit(solution)/shard_map/pallas_call | solution.py:191
  120.7 3.1 %collective-permute-done.15.second_ref = bf16[128,2048]{1,0:T(8,128)(2,1)S(1)} collective-permute-done((bf16[128,2048]{1,0:T(8,128)(2,1)S(1)}, bf16[128,2048]{1,0:T(8,128)(2,1)S(1)}, u32[]{:S(2)}, u32[]{:S(2)}) %collective-permute-start.15) | collective-permute-done | bytes 524320 | tf_op jit(solution)/shard_map/ppermute | solution.py:180
  123.9 4.2 %shard_map.126 = (bf16[128,2048]{1,0:T(8,128)(2,1)S(1)}, bf16[128,2048]{1,0:T(8,128)(2,1)S(1)}) custom-call(s32[1]{0:T(128)} %bitcast.index_ref, bf16[128,2048]{1,0:T(8,128)(2,1)S(1)} %collective-permute-done.14.first_ref, bf16[128,2048]{1,0:T(8,128)(2,1)S(1)} %collective-permute-done.15.second_ref, bf16[8,144,128]{2,1,0:T(8,128)(2,1)S(1)} %copy-done, ...), custom_call_target="tpu_custom_call" | custom-call | flops 3221225472 | bytes 13934596 | tf_op jit(solution)/shard_map/pallas_call | solution.py:191
  128.2 2.0 %collective-permute-start.16 = (bf16[128,2048]{1,0:T(8,128)(2,1)S(1)}, bf16[128,2048]{1,0:T(8,128)(2,1)S(1)}, u32[]{:S(2)}, u32[]{:S(2)}) collective-permute-start(bf16[128,2048]{1,0:T(8,128)(2,1)S(1)} %get-tuple-element.38), channel_id=1, source_target_pairs={{0,4},{1,5},{2,6},{3,7},{4,0},{5,1},{6,2},{7,3},{8,12},{9,13},{10,... | collective-permute-start | bytes 1572872 | tf_op jit(solution)/shard_map/ppermute | solution.py:180
  130.3 2.7 %collective-permute-start.8 = (bf16[128,2048]{1,0:T(8,128)(2,1)S(1)}, bf16[128,2048]{1,0:T(8,128)(2,1)S(1)}, u32[]{:S(2)}, u32[]{:S(2)}) collective-permute-start(bf16[128,2048]{1,0:T(8,128)(2,1)S(1)} %add_convert_fusion.3), channel_id=1, source_target_pairs={{0,12},{1,13},{2,14},{3,15},{4,8},{5,9},{6,10},{7,11},{8,4},{9,5},... | collective-permute-start | bytes 1572872 | tf_op jit(solution)/shard_map/ppermute | solution.py:180
  133.0 3.2 %collective-permute-done.11 = bf16[128,2048]{1,0:T(8,128)(2,1)S(1)} collective-permute-done((bf16[128,2048]{1,0:T(8,128)(2,1)S(1)}, bf16[128,2048]{1,0:T(8,128)(2,1)S(1)}, u32[]{:S(2)}, u32[]{:S(2)}) %collective-permute-start.11) | collective-permute-done | bytes 524320 | tf_op jit(solution)/shard_map/ppermute | solution.py:180
  136.4 1.9 %collective-permute-start.12 = (bf16[128,2048]{1,0:T(8,128)(2,1)S(1)}, bf16[128,2048]{1,0:T(8,128)(2,1)S(1)}, u32[]{:S(2)}, u32[]{:S(2)}) collective-permute-start(bf16[128,2048]{1,0:T(8,128)(2,1)S(1)} %add_convert_fusion.2), channel_id=1, source_target_pairs={{0,8},{1,9},{2,10},{3,11},{4,12},{5,13},{6,14},{7,15},{8,0},{9,1},... | collective-permute-start | bytes 1572872 | tf_op jit(solution)/shard_map/ppermute | solution.py:180
  138.2 5.4 %collective-permute-done.17 = bf16[128,2048]{1,0:T(8,128)(2,1)S(1)} collective-permute-done((bf16[128,2048]{1,0:T(8,128)(2,1)S(1)}, bf16[128,2048]{1,0:T(8,128)(2,1)S(1)}, u32[]{:S(2)}, u32[]{:S(2)}) %collective-permute-start.17) | collective-permute-done | bytes 524320 | tf_op jit(solution)/shard_map/ppermute | solution.py:180
  143.8 0.8 collective-permute-start.18
  144.6 30.6 %collective-permute-done.16 = bf16[128,2048]{1,0:T(8,128)(2,1)S(1)} collective-permute-done((bf16[128,2048]{1,0:T(8,128)(2,1)S(1)}, bf16[128,2048]{1,0:T(8,128)(2,1)S(1)}, u32[]{:S(2)}, u32[]{:S(2)}) %collective-permute-start.16) | collective-permute-done | bytes 524320 | tf_op jit(solution)/shard_map/ppermute | solution.py:180
  175.2 2.0 %collective-permute-done.12 = bf16[128,2048]{1,0:T(8,128)(2,1)S(1)} collective-permute-done((bf16[128,2048]{1,0:T(8,128)(2,1)S(1)}, bf16[128,2048]{1,0:T(8,128)(2,1)S(1)}, u32[]{:S(2)}, u32[]{:S(2)}) %collective-permute-start.12) | collective-permute-done | bytes 524320 | tf_op jit(solution)/shard_map/ppermute | solution.py:180
  177.2 1.3 add_convert_fusion
  (33 shorter events, 2.0 us)
Async XLA Ops:
  0.0 32.0 %copy-start.5 = (s32[128,1]{0,1:T(1,128)S(1)}, s32[128,1]{0,1:T(1,128)}, u32[]{:S(2)}) copy-start(s32[128,1]{0,1:T(1,128)} %param.21) | copy-start | bytes 1540
  29.7 2.3 %collective-permute-start = (bf16[8,128,384]{2,1,0:T(8,128)(2,1)S(1)}, bf16[8,128,384]{2,1,0:T(8,128)(2,1)S(1)}, u32[]{:S(2)}, u32[]{:S(2)}) collective-permute-start(bf16[8,128,384]{2,1,0:T(8,128)(2,1)S(1)} %all_to_all.10.own_ref), channel_id=1, source_target_pairs={{0,1},{1,0},{2,3},{3,2},{4,5},{5,4},{6,7},{7,6},{8,9},{9,8},{10,11... | collective-permute-start | bytes 2359304 | tf_op jit(solution)/shard_map/ppermute | solution.py:180
  29.7 44.8 %collective-permute-start.4 = (bf16[2048,512]{1,0:T(8,128)(2,1)}, bf16[2048,512]{1,0:T(8,128)(2,1)}, u32[]{:S(2)}, u32[]{:S(2)}) collective-permute-start(bf16[2048,512]{1,0:T(8,128)(2,1)} %bitcast.6), channel_id=1, source_target_pairs={{0,1},{1,0},{2,3},{3,2},{4,5},{5,4},{6,7},{7,6},{8,9},{9,8},{10,11... | collective-permute-start | bytes 6291464 | tf_op jit(solution)/shard_map/ppermute | solution.py:180
  30.2 44.3 %collective-permute-start.6 = (bf16[512,2048]{1,0:T(8,128)(2,1)}, bf16[512,2048]{1,0:T(8,128)(2,1)}, u32[]{:S(2)}, u32[]{:S(2)}) collective-permute-start(bf16[512,2048]{1,0:T(8,128)(2,1)} %bitcast.8), channel_id=1, source_target_pairs={{0,1},{1,0},{2,3},{3,2},{4,5},{5,4},{6,7},{7,6},{8,9},{9,8},{10,11... | collective-permute-start | bytes 6291464 | tf_op jit(solution)/shard_map/ppermute | solution.py:180
  30.2 26.6 %collective-permute-start.3 = (bf16[2048,256]{1,0:T(8,128)(2,1)}, bf16[2048,256]{1,0:T(8,128)(2,1)}, u32[]{:S(2)}, u32[]{:S(2)}) collective-permute-start(bf16[2048,256]{1,0:T(8,128)(2,1)} %refs_0_.1), channel_id=1, source_target_pairs={{0,1},{1,0},{2,3},{3,2},{4,5},{5,4},{6,7},{7,6},{8,9},{9,8},{10,11... | collective-permute-start | bytes 3145736 | tf_op jit(solution)/shard_map/ppermute | solution.py:180
  30.7 26.7 %collective-permute-start.5 = (bf16[2048,256]{1,0:T(8,128)(2,1)}, bf16[2048,256]{1,0:T(8,128)(2,1)}, u32[]{:S(2)}, u32[]{:S(2)}) collective-permute-start(bf16[2048,256]{1,0:T(8,128)(2,1)} %refs_2_.1), channel_id=1, source_target_pairs={{0,1},{1,0},{2,3},{3,2},{4,5},{5,4},{6,7},{7,6},{8,9},{9,8},{10,11... | collective-permute-start | bytes 3145736 | tf_op jit(solution)/shard_map/ppermute | solution.py:180
  50.2 22.6 %copy-start.1 = (bf16[1,2048,512]{2,1,0:T(8,128)(2,1)S(1)}, bf16[1,2048,512]{2,1,0:T(8,128)(2,1)}, u32[]{:S(2)}) copy-start(bf16[1,2048,512]{2,1,0:T(8,128)(2,1)} %param.22) | copy-start | bytes 6291460
  50.2 22.6 %copy-start.2 = (bf16[1,512,2048]{2,1,0:T(8,128)(2,1)S(1)}, bf16[1,512,2048]{2,1,0:T(8,128)(2,1)}, u32[]{:S(2)}) copy-start(bf16[1,512,2048]{2,1,0:T(8,128)(2,1)} %param.23) | copy-start | bytes 6291460
  55.2 16.9 %collective-permute-start.1 = (bf16[128,2048]{1,0:T(8,128)(2,1)}, bf16[128,2048]{1,0:T(8,128)(2,1)S(1)}, u32[]{:S(2)}, u32[]{:S(2)}) collective-permute-start(bf16[128,2048]{1,0:T(8,128)(2,1)} %get-tuple-element.24.first_ref), channel_id=1, source_target_pairs={{0,12},{1,13},{2,14},{3,15},{4,8},{5,9},{6,10},{7,11},{8,4},{9,5},... | collective-permute-start | bytes 1572872 | tf_op jit(solution)/shard_map/ppermute | solution.py:180
  56.8 44.7 %collective-permute-start.9 = (bf16[128,2048]{1,0:T(8,128)(2,1)}, bf16[128,2048]{1,0:T(8,128)(2,1)S(1)}, u32[]{:S(2)}, u32[]{:S(2)}) collective-permute-start(bf16[128,2048]{1,0:T(8,128)(2,1)} %get-tuple-element.24.first_ref), channel_id=1, source_target_pairs={{0,8},{1,9},{2,10},{3,11},{4,12},{5,13},{6,14},{7,15},{8,0},{9,1},... | collective-permute-start | bytes 1572872 | tf_op jit(solution)/shard_map/ppermute | solution.py:180
  57.4 44.8 %collective-permute-start.13 = (bf16[128,2048]{1,0:T(8,128)(2,1)}, bf16[128,2048]{1,0:T(8,128)(2,1)S(1)}, u32[]{:S(2)}, u32[]{:S(2)}) collective-permute-start(bf16[128,2048]{1,0:T(8,128)(2,1)} %get-tuple-element.24.first_ref), channel_id=1, source_target_pairs={{0,2},{1,3},{2,0},{3,1},{4,6},{5,7},{6,4},{7,5},{8,10},{9,11},{10,... | collective-permute-start | bytes 1572872 | tf_op jit(solution)/shard_map/ppermute | solution.py:180
  72.2 34.1 %collective-permute-start.2 = (bf16[128,2048]{1,0:T(8,128)(2,1)S(1)}, bf16[128,2048]{1,0:T(8,128)(2,1)S(1)}, u32[]{:S(2)}, u32[]{:S(2)}) collective-permute-start(bf16[128,2048]{1,0:T(8,128)(2,1)S(1)} %collective-permute-done.1.first_ref), channel_id=1, source_target_pairs={{0,2},{1,3},{2,0},{3,1},{4,6},{5,7},{6,4},{7,5},{8,10},{9,11},{10,... | collective-permute-start | bytes 1572872 | tf_op jit(solution)/shard_map/ppermute | solution.py:180
  74.5 3.0 %copy-start.3 = (bf16[128,2048]{1,0:T(8,128)(2,1)S(1)}, bf16[128,2048]{1,0:T(8,128)(2,1)}, u32[]{:S(2)}) copy-start(bf16[128,2048]{1,0:T(8,128)(2,1)} %get-tuple-element.24.first_ref) | copy-start | bytes 1572868
  74.5 27.8 %copy-start = (bf16[8,144,128]{2,1,0:T(8,128)(2,1)S(1)}, bf16[8,144,128]{2,1,0:T(8,128)(2,1)}, u32[]{:S(2)}) copy-start(bf16[8,144,128]{2,1,0:T(8,128)(2,1)} %all_to_all.11.back_ref) | copy-start | bytes 884740
  74.5 27.8 %copy-start.4 = (bf16[2048,2]{0,1:T(2,128)(2,1)S(1)}, bf16[2048,2]{0,1:T(2,128)(2,1)}, u32[]{:S(2)}) copy-start(bf16[2048,2]{0,1:T(2,128)(2,1)} %param.20) | copy-start | bytes 24580
  77.5 43.2 %collective-permute-start.14 = (bf16[128,2048]{1,0:T(8,128)(2,1)S(1)}, bf16[128,2048]{1,0:T(8,128)(2,1)S(1)}, u32[]{:S(2)}, u32[]{:S(2)}) collective-permute-start(bf16[128,2048]{1,0:T(8,128)(2,1)S(1)} %copy-done.3), channel_id=1, source_target_pairs={{0,4},{1,5},{2,6},{3,7},{4,0},{5,1},{6,2},{7,3},{8,12},{9,13},{10,... | collective-permute-start | bytes 1572872 | tf_op jit(solution)/shard_map/ppermute | solution.py:180
  101.5 14.8 %collective-permute-start.10 = (bf16[128,2048]{1,0:T(8,128)(2,1)S(1)}, bf16[128,2048]{1,0:T(8,128)(2,1)S(1)}, u32[]{:S(2)}, u32[]{:S(2)}) collective-permute-start(bf16[128,2048]{1,0:T(8,128)(2,1)S(1)} %collective-permute-done.9.first_ref), channel_id=1, source_target_pairs={{0,2},{1,3},{2,0},{3,1},{4,6},{5,7},{6,4},{7,5},{8,10},{9,11},{10,... | collective-permute-start | bytes 1572872 | tf_op jit(solution)/shard_map/ppermute | solution.py:180
  102.3 21.6 %collective-permute-start.15 = (bf16[128,2048]{1,0:T(8,128)(2,1)S(1)}, bf16[128,2048]{1,0:T(8,128)(2,1)S(1)}, u32[]{:S(2)}, u32[]{:S(2)}) collective-permute-start(bf16[128,2048]{1,0:T(8,128)(2,1)S(1)} %collective-permute-done.13.second_ref), channel_id=1, source_target_pairs={{0,4},{1,5},{2,6},{3,7},{4,0},{5,1},{6,2},{7,3},{8,12},{9,13},{10,... | collective-permute-start | bytes 1572872 | tf_op jit(solution)/shard_map/ppermute | solution.py:180
  110.2 20.0 %collective-permute-start.7 = (bf16[128,2048]{1,0:T(8,128)(2,1)S(1)}, bf16[128,2048]{1,0:T(8,128)(2,1)S(1)}, u32[]{:S(2)}, u32[]{:S(2)}) collective-permute-start(bf16[128,2048]{1,0:T(8,128)(2,1)S(1)} %get-tuple-element.34), channel_id=1, source_target_pairs={{0,2},{1,3},{2,0},{3,1},{4,6},{5,7},{6,4},{7,5},{8,10},{9,11},{10,... | collective-permute-start | bytes 1572872 | tf_op jit(solution)/shard_map/ppermute | solution.py:180
  120.2 16.0 %collective-permute-start.11 = (bf16[128,2048]{1,0:T(8,128)(2,1)S(1)}, bf16[128,2048]{1,0:T(8,128)(2,1)S(1)}, u32[]{:S(2)}, u32[]{:S(2)}) collective-permute-start(bf16[128,2048]{1,0:T(8,128)(2,1)S(1)} %get-tuple-element.36), channel_id=1, source_target_pairs={{0,2},{1,3},{2,0},{3,1},{4,6},{5,7},{6,4},{7,5},{8,10},{9,11},{10,... | collective-permute-start | bytes 1572872 | tf_op jit(solution)/shard_map/ppermute | solution.py:180
  128.1 15.6 %collective-permute-start.17 = (bf16[128,2048]{1,0:T(8,128)(2,1)S(1)}, bf16[128,2048]{1,0:T(8,128)(2,1)S(1)}, u32[]{:S(2)}, u32[]{:S(2)}) collective-permute-start(bf16[128,2048]{1,0:T(8,128)(2,1)S(1)} %get-tuple-element.40), channel_id=1, source_target_pairs={{0,4},{1,5},{2,6},{3,7},{4,0},{5,1},{6,2},{7,3},{8,12},{9,13},{10,... | collective-permute-start | bytes 1572872 | tf_op jit(solution)/shard_map/ppermute | solution.py:180
  128.2 47.0 %collective-permute-start.16 = (bf16[128,2048]{1,0:T(8,128)(2,1)S(1)}, bf16[128,2048]{1,0:T(8,128)(2,1)S(1)}, u32[]{:S(2)}, u32[]{:S(2)}) collective-permute-start(bf16[128,2048]{1,0:T(8,128)(2,1)S(1)} %get-tuple-element.38), channel_id=1, source_target_pairs={{0,4},{1,5},{2,6},{3,7},{4,0},{5,1},{6,2},{7,3},{8,12},{9,13},{10,... | collective-permute-start | bytes 1572872 | tf_op jit(solution)/shard_map/ppermute | solution.py:180
  130.3 44.9 %collective-permute-start.8 = (bf16[128,2048]{1,0:T(8,128)(2,1)S(1)}, bf16[128,2048]{1,0:T(8,128)(2,1)S(1)}, u32[]{:S(2)}, u32[]{:S(2)}) collective-permute-start(bf16[128,2048]{1,0:T(8,128)(2,1)S(1)} %add_convert_fusion.3), channel_id=1, source_target_pairs={{0,12},{1,13},{2,14},{3,15},{4,8},{5,9},{6,10},{7,11},{8,4},{9,5},... | collective-permute-start | bytes 1572872 | tf_op jit(solution)/shard_map/ppermute | solution.py:180
  136.4 40.8 %collective-permute-start.12 = (bf16[128,2048]{1,0:T(8,128)(2,1)S(1)}, bf16[128,2048]{1,0:T(8,128)(2,1)S(1)}, u32[]{:S(2)}, u32[]{:S(2)}) collective-permute-start(bf16[128,2048]{1,0:T(8,128)(2,1)S(1)} %add_convert_fusion.2), channel_id=1, source_target_pairs={{0,8},{1,9},{2,10},{3,11},{4,12},{5,13},{6,14},{7,15},{8,0},{9,1},... | collective-permute-start | bytes 1572872 | tf_op jit(solution)/shard_map/ppermute | solution.py:180
  143.8 33.4 %collective-permute-start.18 = (bf16[128,2048]{1,0:T(8,128)(2,1)S(1)}, bf16[128,2048]{1,0:T(8,128)(2,1)S(1)}, u32[]{:S(2)}, u32[]{:S(2)}) collective-permute-start(bf16[128,2048]{1,0:T(8,128)(2,1)S(1)} %add_convert_fusion.1), channel_id=1, source_target_pairs={{0,2},{1,3},{2,0},{3,1},{4,6},{5,7},{6,4},{7,5},{8,10},{9,11},{10,... | collective-permute-start | bytes 1572872 | tf_op jit(solution)/shard_map/ppermute | solution.py:180

commit v2 on v1

--- a/solution.py
+++ b/solution.py
@@ -278,28 +278,35 @@
         out_ref[block, rows:, :] = id_rows
 
 
-def project_kernel(back_ref, weight_ref, resid_ref, gain_ref, mixed_ref, normed_ref, held, resid, sems):
-    rows = resid_ref.shape[0]
+def project_kernel(
+    back_ref, weight_ref, resid_ref, gain_ref, mixed_ref, normed_ref, held, back, resid, sems
+):
+    rows, width = resid_ref.shape
     pieces = held.shape[0]
-    depth = held.shape[1]
+    step = width // pieces
     copies = [
-        pltpu.make_async_copy(weight_ref.at[pl.ds(at * depth, depth), :], held.at[at], sems.at[at])
+        pltpu.make_async_copy(back_ref, back, sems.at[pieces]),
+        pltpu.make_async_copy(resid_ref, resid, sems.at[pieces + 1]),
+    ] + [
+        pltpu.make_async_copy(weight_ref.at[:, pl.ds(at * step, step)], held.at[at], sems.at[at])
         for at in range(pieces)
     ]
-    copies.append(pltpu.make_async_copy(resid_ref, resid, sems.at[pieces]))
-    for copy in copies[-1:] + copies[:-1]:
+    for copy in copies:
         copy.start()
-    attn = jnp.concatenate([back_ref[head, :rows, :] for head in range(back_ref.shape[0])], axis=1)
-    copies[-1].wait()
-    mixed = resid[...].astype(jnp.float32)
+    copies[0].wait()
+    attn = jnp.concatenate([back[head, :rows, :] for head in range(back.shape[0])], axis=1)
+    copies[1].wait()
+    squares = jnp.zeros((rows, 1), jnp.float32)
     for at in range(pieces):
-        copies[at].wait()
-        mixed = mixed + jnp.dot(
-            attn[:, at * depth : (at + 1) * depth], held[at], preferred_element_type=jnp.float32
-        )
-    mixed_ref[...] = mixed
-    scale = lax.rsqrt(jnp.mean(mixed * mixed, axis=1, keepdims=True) + EPSILON)
-    normed_ref[...] = (mixed * scale * gain_ref[...]).astype(jnp.bfloat16)
+        span = slice(at * step, (at + 1) * step)
+        copies[at + 2].wait()
+        mixed = resid[:, span].astype(jnp.float32) + jnp.dot(
+            attn, held[at], preferred_element_type=jnp.float32
+        )
+        mixed_ref[:, span] = mixed
+        squares = squares + jnp.sum(mixed * mixed, axis=1, keepdims=True)
+    scale = lax.rsqrt(squares / width + EPSILON)
+    normed_ref[...] = (mixed_ref[...] * scale * gain_ref[...]).astype(jnp.bfloat16)
 
 
 def mixture_kernel(
@@ -417,20 +424,21 @@
         expert_ids.reshape(1, rows),
     )
     back = exchange(out)
-    pieces = heads // 2
+    pieces = 4
     mixed, normed = call(
         project_kernel,
         [pltpu.VMEM((rows, width), jnp.float32), shape((rows, width), jnp.bfloat16)],
-        [VMEM, HBM, HBM, VMEM],
+        [HBM, HBM, HBM, VMEM],
         2 * out_proj.size * rows,
         58,
         back,
         out_proj,
         resid,
         norm_gain.reshape(1, width),
-        copies=pieces + 1,
+        copies=pieces + 2,
         scratch=[
-            pltpu.VMEM((pieces, out_proj.shape[0] // pieces, width), out_proj.dtype),
+            pltpu.VMEM((pieces, out_proj.shape[0], width // pieces), out_proj.dtype),
+            pltpu.VMEM(back.shape, back.dtype),
             pltpu.VMEM(resid.shape, resid.dtype),
         ],
     )

time: 179 us -> 179 us (level)
  no operation moved by 1% of the time
where the time goes in v2:
time: 179 us
  waiting for transfers between devices  68.3 us (38%)
  blocking collectives  41.6 us (23%)
  starting transfers between devices  34.8 us (19%)
  Pallas kernels  32.1 us (18%)
    ppermute x19, waiting for transfers between devices, swap(): lax.ppermute(array, 'ctx', [(i, i ^ mask) for i in range(lax.axis_size('c...  68.3 us
    ppermute x19, starting transfers between devices, swap(): lax.ppermute(array, 'ctx', [(i, i ^ mask) for i in range(lax.axis_size('c...  34.8 us
    pallas_call x9, Pallas kernels, call(): pl.pallas_call(kernel, out_shape=outs, in_specs=specs, out_specs=[VMEM] *...  32.1 us
    all_to_all x1, blocking collectives, body_by_pairs(): own = exchange(packed)  27.5 us
    all_to_all x1, blocking collectives, body_by_pairs(): back = exchange(out)  14.1 us
  transfers between devices with their start and end apart: 19, of which 9 were waited for; matrix products, arithmetic and copies ran while one was open for 0% of the time, Pallas kernels for 17%

profile of v2, /device:TPU:0, one launch (start us, length us, event | category | flops | bytes accessed | tf_op | source)
XLA Modules:
  0.0 178.7 jit_solution(9072400583879003388)
XLA Ops:
  0.0 2.2 %shard_map.118 = bf16[8,128,384]{2,1,0:T(8,128)(2,1)} custom-call(bf16[128,1024]{1,0:T(8,128)(2,1)} %query_ref.1, bf16[128,1024]{1,0:T(8,128)(2,1)} %key_ref.1, bf16[128,1024]{1,0:T(8,128)(2,1)} %value_ref.1), custom_call_target="tpu_custom_call" | custom-call | bytes 786432 | tf_op jit(solution)/shard_map/pallas_call | solution.py:191
  2.2 27.5 %all_to_all.10.own_ref = bf16[8,128,384]{2,1,0:T(8,128)(2,1)S(1)} all-to-all(bf16[8,128,384]{2,1,0:T(8,128)(2,1)} %shard_map.118), channel_id=1, replica_groups={{0,2,4,6,8,10,12,14},{1,3,5,7,9,11,13,15},{16,18,20,22,24,26,28,30},{17..., dimensions={0} | all-to-all | bytes 1572864 | tf_op jit(solution)/shard_map/all_to_all | solution.py:408
  30.7 1.3 collective-permute-done.other_ref
  32.0 4.1 %shard_map.119 = bf16[8,144,128]{2,1,0:T(8,128)(2,1)S(1)} custom-call(s32[1]{0:T(128)} %bitcast.index_ref, bf16[8,128,384]{2,1,0:T(8,128)(2,1)S(1)} %all_to_all.10.own_ref, bf16[8,128,384]{2,1,0:T(8,128)(2,1)S(1)} %collective-permute-done.other_ref, s32[1,128]{1,0:T(1,128)S(1)} %bitcast.14), custom_call_target="tpu_custom_call" | custom-call | flops 1000000000 | bytes 1573380 | tf_op jit(solution)/shard_map/pallas_call | solution.py:191
  36.1 14.1 %all_to_all.11.back_ref = bf16[8,144,128]{2,1,0:T(8,128)(2,1)} all-to-all(bf16[8,144,128]{2,1,0:T(8,128)(2,1)S(1)} %shard_map.119), channel_id=1, replica_groups={{0,2,4,6,8,10,12,14},{1,3,5,7,9,11,13,15},{16,18,20,22,24,26,28,30},{17..., dimensions={0} | all-to-all | bytes 589824 | tf_op jit(solution)/shard_map/all_to_all | solution.py:426
  50.2 5.2 %shard_map.120 = (f32[128,2048]{1,0:T(8,128)S(1)}, bf16[128,2048]{1,0:T(8,128)(2,1)}) custom-call(bf16[8,144,128]{2,1,0:T(8,128)(2,1)} %all_to_all.11.back_ref, bf16[1024,2048]{1,0:T(8,128)(2,1)} %weight_ref.1, bf16[128,2048]{1,0:T(8,128)(2,1)} %resid_ref.1, f32[1,2048]{1,0:T(1,128)} %bitcast.15), custom_call_target="tpu_custom_call" | custom-call | flops 536870912 | bytes 5021696 | tf_op jit(solution)/shard_map/pallas_call | solution.py:191
  55.5 1.5 collective-permute-start.1
  57.0 0.7 collective-permute-start.9
  57.6 0.5 collective-permute-start.13
  58.2 14.2 %collective-permute-done.1.first_ref = bf16[128,2048]{1,0:T(8,128)(2,1)S(1)} collective-permute-done((bf16[128,2048]{1,0:T(8,128)(2,1)}, bf16[128,2048]{1,0:T(8,128)(2,1)S(1)}, u32[]{:S(2)}, u32[]{:S(2)}) %collective-permute-start.1) | collective-permute-done | bytes 524320 | tf_op jit(solution)/shard_map/ppermute | solution.py:180
  72.4 0.7 collective-permute-start.2
  73.1 1.6 shard_map.121
  74.7 3.0 %shard_map.122 = (bf16[2048,256]{1,0:T(8,128)(2,1)S(1)}, bf16[2048,512]{1,0:T(8,128)(2,1)S(1)}, bf16[2048,256]{1,0:T(8,128)(2,1)S(1)}, bf16[512,2048]{1,0:T(8,128)(2,1)S(1)}) custom-call(bf16[2048,256]{1,0:T(8,128)(2,1)} %collective-permute-done.3.refs_0_, bf16[2048,512]{1,0:T(8,128)(2,1)} %collective-permute-done.4.refs_1_, ...), custom_call_target="tpu_custom_call" | custom-call | bytes 6291456 | tf_op jit(solution)/shard_map/pallas_call | solution.py:191
  77.7 20.3 %collective-permute-start.14 = (bf16[128,2048]{1,0:T(8,128)(2,1)S(1)}, bf16[128,2048]{1,0:T(8,128)(2,1)S(1)}, u32[]{:S(2)}, u32[]{:S(2)}) collective-permute-start(bf16[128,2048]{1,0:T(8,128)(2,1)S(1)} %copy-done.3), channel_id=1, source_target_pairs={{0,4},{1,5},{2,6},{3,7},{4,0},{5,1},{6,2},{7,3},{8,12},{9,13},{10,... | collective-permute-start | bytes 1572872 | tf_op jit(solution)/shard_map/ppermute | solution.py:180
  98.1 3.7 %collective-permute-done.9.first_ref = bf16[128,2048]{1,0:T(8,128)(2,1)S(1)} collective-permute-done((bf16[128,2048]{1,0:T(8,128)(2,1)}, bf16[128,2048]{1,0:T(8,128)(2,1)S(1)}, u32[]{:S(2)}, u32[]{:S(2)}) %collective-permute-start.9) | collective-permute-done | bytes 524320 | tf_op jit(solution)/shard_map/ppermute | solution.py:180
  101.7 0.7 collective-permute-start.10
  102.5 4.0 %shard_map.125 = (bf16[128,2048]{1,0:T(8,128)(2,1)S(1)}, bf16[128,2048]{1,0:T(8,128)(2,1)S(1)}) custom-call(s32[1]{0:T(128)} %bitcast.index_ref, bf16[128,2048]{1,0:T(8,128)(2,1)S(1)} %copy-done.3, bf16[128,2048]{1,0:T(8,128)(2,1)S(1)} %collective-permute-done.13.second_ref, bf16[8,144,128]{2,1,0:T(8,128)(2,1)S(1)} %copy-done, bf16[2,2048]{1,0:T(2,128)(2,1)S(1)} %bitcast.10, ...), custom_call_target="tpu_custom_call" | custom-call | flops 3221225472 | bytes 13934596 | tf_op jit(solution)/shard_map/pallas_call | solution.py:191
  106.5 4.0 %shard_map.123 = (bf16[128,2048]{1,0:T(8,128)(2,1)S(1)}, bf16[128,2048]{1,0:T(8,128)(2,1)S(1)}) custom-call(s32[1]{0:T(128)} %bitcast.index_ref, bf16[128,2048]{1,0:T(8,128)(2,1)S(1)} %collective-permute-done.1.first_ref, bf16[128,2048]{1,0:T(8,128)(2,1)S(1)} %collective-permute-done.2.second_ref, bf16[8,144,128]{2,1,0:T(8,128)(2,1)S(1)} %copy-done, ...), custom_call_target="tpu_custom_call" | custom-call | flops 3221225472 | bytes 13934596 | tf_op jit(solution)/shard_map/pallas_call | solution.py:191
  110.4 1.3 collective-permute-start.7
  111.8 4.8 %collective-permute-done.10.second_ref = bf16[128,2048]{1,0:T(8,128)(2,1)S(1)} collective-permute-done((bf16[128,2048]{1,0:T(8,128)(2,1)S(1)}, bf16[128,2048]{1,0:T(8,128)(2,1)S(1)}, u32[]{:S(2)}, u32[]{:S(2)}) %collective-permute-start.10) | collective-permute-done | bytes 524320 | tf_op jit(solution)/shard_map/ppermute | solution.py:180
  116.5 3.9 %shard_map.124 = (bf16[128,2048]{1,0:T(8,128)(2,1)S(1)}, bf16[128,2048]{1,0:T(8,128)(2,1)S(1)}) custom-call(s32[1]{0:T(128)} %bitcast.index_ref, bf16[128,2048]{1,0:T(8,128)(2,1)S(1)} %collective-permute-done.9.first_ref, bf16[128,2048]{1,0:T(8,128)(2,1)S(1)} %collective-permute-done.10.second_ref, bf16[8,144,128]{2,1,0:T(8,128)(2,1)S(1)} %copy-done, ...), custom_call_target="tpu_custom_call" | custom-call | flops 3221225472 | bytes 13934596 | tf_op jit(solution)/shard_map/pallas_call | solution.py:191
  120.9 3.2 %collective-permute-done.15.second_ref = bf16[128,2048]{1,0:T(8,128)(2,1)S(1)} collective-permute-done((bf16[128,2048]{1,0:T(8,128)(2,1)S(1)}, bf16[128,2048]{1,0:T(8,128)(2,1)S(1)}, u32[]{:S(2)}, u32[]{:S(2)}) %collective-permute-start.15) | collective-permute-done | bytes 524320 | tf_op jit(solution)/shard_map/ppermute | solution.py:180
  124.1 4.2 %shard_map.126 = (bf16[128,2048]{1,0:T(8,128)(2,1)S(1)}, bf16[128,2048]{1,0:T(8,128)(2,1)S(1)}) custom-call(s32[1]{0:T(128)} %bitcast.index_ref, bf16[128,2048]{1,0:T(8,128)(2,1)S(1)} %collective-permute-done.14.first_ref, bf16[128,2048]{1,0:T(8,128)(2,1)S(1)} %collective-permute-done.15.second_ref, bf16[8,144,128]{2,1,0:T(8,128)(2,1)S(1)} %copy-done, ...), custom_call_target="tpu_custom_call" | custom-call | flops 3221225472 | bytes 13934596 | tf_op jit(solution)/shard_map/pallas_call | solution.py:191
  128.4 2.0 %collective-permute-start.16 = (bf16[128,2048]{1,0:T(8,128)(2,1)S(1)}, bf16[128,2048]{1,0:T(8,128)(2,1)S(1)}, u32[]{:S(2)}, u32[]{:S(2)}) collective-permute-start(bf16[128,2048]{1,0:T(8,128)(2,1)S(1)} %get-tuple-element.38), channel_id=1, source_target_pairs={{0,4},{1,5},{2,6},{3,7},{4,0},{5,1},{6,2},{7,3},{8,12},{9,13},{10,... | collective-permute-start | bytes 1572872 | tf_op jit(solution)/shard_map/ppermute | solution.py:180
  130.5 2.7 %collective-permute-start.8 = (bf16[128,2048]{1,0:T(8,128)(2,1)S(1)}, bf16[128,2048]{1,0:T(8,128)(2,1)S(1)}, u32[]{:S(2)}, u32[]{:S(2)}) collective-permute-start(bf16[128,2048]{1,0:T(8,128)(2,1)S(1)} %add_convert_fusion.3), channel_id=1, source_target_pairs={{0,12},{1,13},{2,14},{3,15},{4,8},{5,9},{6,10},{7,11},{8,4},{9,5},... | collective-permute-start | bytes 1572872 | tf_op jit(solution)/shard_map/ppermute | solution.py:180
  133.2 3.2 %collective-permute-done.11 = bf16[128,2048]{1,0:T(8,128)(2,1)S(1)} collective-permute-done((bf16[128,2048]{1,0:T(8,128)(2,1)S(1)}, bf16[128,2048]{1,0:T(8,128)(2,1)S(1)}, u32[]{:S(2)}, u32[]{:S(2)}) %collective-permute-start.11) | collective-permute-done | bytes 524320 | tf_op jit(solution)/shard_map/ppermute | solution.py:180
  136.6 1.9 %collective-permute-start.12 = (bf16[128,2048]{1,0:T(8,128)(2,1)S(1)}, bf16[128,2048]{1,0:T(8,128)(2,1)S(1)}, u32[]{:S(2)}, u32[]{:S(2)}) collective-permute-start(bf16[128,2048]{1,0:T(8,128)(2,1)S(1)} %add_convert_fusion.2), channel_id=1, source_target_pairs={{0,8},{1,9},{2,10},{3,11},{4,12},{5,13},{6,14},{7,15},{8,0},{9,1},... | collective-permute-start | bytes 1572872 | tf_op jit(solution)/shard_map/ppermute | solution.py:180
  138.5 5.4 %collective-permute-done.17 = bf16[128,2048]{1,0:T(8,128)(2,1)S(1)} collective-permute-done((bf16[128,2048]{1,0:T(8,128)(2,1)S(1)}, bf16[128,2048]{1,0:T(8,128)(2,1)S(1)}, u32[]{:S(2)}, u32[]{:S(2)}) %collective-permute-start.17) | collective-permute-done | bytes 524320 | tf_op jit(solution)/shard_map/ppermute | solution.py:180
  144.0 0.8 collective-permute-start.18
  144.8 30.6 %collective-permute-done.16 = bf16[128,2048]{1,0:T(8,128)(2,1)S(1)} collective-permute-done((bf16[128,2048]{1,0:T(8,128)(2,1)S(1)}, bf16[128,2048]{1,0:T(8,128)(2,1)S(1)}, u32[]{:S(2)}, u32[]{:S(2)}) %collective-permute-start.16) | collective-permute-done | bytes 524320 | tf_op jit(solution)/shard_map/ppermute | solution.py:180
  175.4 2.0 %collective-permute-done.12 = bf16[128,2048]{1,0:T(8,128)(2,1)S(1)} collective-permute-done((bf16[128,2048]{1,0:T(8,128)(2,1)S(1)}, bf16[128,2048]{1,0:T(8,128)(2,1)S(1)}, u32[]{:S(2)}, u32[]{:S(2)}) %collective-permute-start.12) | collective-permute-done | bytes 524320 | tf_op jit(solution)/shard_map/ppermute | solution.py:180
  177.4 1.3 add_convert_fusion
  (33 shorter events, 2.0 us)
Async XLA Ops:
  0.0 32.0 %copy-start.5 = (s32[128,1]{0,1:T(1,128)S(1)}, s32[128,1]{0,1:T(1,128)}, u32[]{:S(2)}) copy-start(s32[128,1]{0,1:T(1,128)} %param.21) | copy-start | bytes 1540
  29.7 2.3 %collective-permute-start = (bf16[8,128,384]{2,1,0:T(8,128)(2,1)S(1)}, bf16[8,128,384]{2,1,0:T(8,128)(2,1)S(1)}, u32[]{:S(2)}, u32[]{:S(2)}) collective-permute-start(bf16[8,128,384]{2,1,0:T(8,128)(2,1)S(1)} %all_to_all.10.own_ref), channel_id=1, source_target_pairs={{0,1},{1,0},{2,3},{3,2},{4,5},{5,4},{6,7},{7,6},{8,9},{9,8},{10,11... | collective-permute-start | bytes 2359304 | tf_op jit(solution)/shard_map/ppermute | solution.py:180
  29.7 45.0 %collective-permute-start.4 = (bf16[2048,512]{1,0:T(8,128)(2,1)}, bf16[2048,512]{1,0:T(8,128)(2,1)}, u32[]{:S(2)}, u32[]{:S(2)}) collective-permute-start(bf16[2048,512]{1,0:T(8,128)(2,1)} %bitcast.6), channel_id=1, source_target_pairs={{0,1},{1,0},{2,3},{3,2},{4,5},{5,4},{6,7},{7,6},{8,9},{9,8},{10,11... | collective-permute-start | bytes 6291464 | tf_op jit(solution)/shard_map/ppermute | solution.py:180
  30.2 44.5 %collective-permute-start.6 = (bf16[512,2048]{1,0:T(8,128)(2,1)}, bf16[512,2048]{1,0:T(8,128)(2,1)}, u32[]{:S(2)}, u32[]{:S(2)}) collective-permute-start(bf16[512,2048]{1,0:T(8,128)(2,1)} %bitcast.8), channel_id=1, source_target_pairs={{0,1},{1,0},{2,3},{3,2},{4,5},{5,4},{6,7},{7,6},{8,9},{9,8},{10,11... | collective-permute-start | bytes 6291464 | tf_op jit(solution)/shard_map/ppermute | solution.py:180
  30.2 26.8 %collective-permute-start.3 = (bf16[2048,256]{1,0:T(8,128)(2,1)}, bf16[2048,256]{1,0:T(8,128)(2,1)}, u32[]{:S(2)}, u32[]{:S(2)}) collective-permute-start(bf16[2048,256]{1,0:T(8,128)(2,1)} %refs_0_.1), channel_id=1, source_target_pairs={{0,1},{1,0},{2,3},{3,2},{4,5},{5,4},{6,7},{7,6},{8,9},{9,8},{10,11... | collective-permute-start | bytes 3145736 | tf_op jit(solution)/shard_map/ppermute | solution.py:180
  30.7 26.9 %collective-permute-start.5 = (bf16[2048,256]{1,0:T(8,128)(2,1)}, bf16[2048,256]{1,0:T(8,128)(2,1)}, u32[]{:S(2)}, u32[]{:S(2)}) collective-permute-start(bf16[2048,256]{1,0:T(8,128)(2,1)} %refs_2_.1), channel_id=1, source_target_pairs={{0,1},{1,0},{2,3},{3,2},{4,5},{5,4},{6,7},{7,6},{8,9},{9,8},{10,11... | collective-permute-start | bytes 3145736 | tf_op jit(solution)/shard_map/ppermute | solution.py:180
  50.2 22.8 %copy-start.1 = (bf16[1,2048,512]{2,1,0:T(8,128)(2,1)S(1)}, bf16[1,2048,512]{2,1,0:T(8,128)(2,1)}, u32[]{:S(2)}) copy-start(bf16[1,2048,512]{2,1,0:T(8,128)(2,1)} %param.22) | copy-start | bytes 6291460
  50.2 22.8 %copy-start.2 = (bf16[1,512,2048]{2,1,0:T(8,128)(2,1)S(1)}, bf16[1,512,2048]{2,1,0:T(8,128)(2,1)}, u32[]{:S(2)}) copy-start(bf16[1,512,2048]{2,1,0:T(8,128)(2,1)} %param.23) | copy-start | bytes 6291460
  55.5 16.9 %collective-permute-start.1 = (bf16[128,2048]{1,0:T(8,128)(2,1)}, bf16[128,2048]{1,0:T(8,128)(2,1)S(1)}, u32[]{:S(2)}, u32[]{:S(2)}) collective-permute-start(bf16[128,2048]{1,0:T(8,128)(2,1)} %get-tuple-element.24.first_ref), channel_id=1, source_target_pairs={{0,12},{1,13},{2,14},{3,15},{4,8},{5,9},{6,10},{7,11},{8,4},{9,5},... | collective-permute-start | bytes 1572872 | tf_op jit(solution)/shard_map/ppermute | solution.py:180
  57.0 44.8 %collective-permute-start.9 = (bf16[128,2048]{1,0:T(8,128)(2,1)}, bf16[128,2048]{1,0:T(8,128)(2,1)S(1)}, u32[]{:S(2)}, u32[]{:S(2)}) collective-permute-start(bf16[128,2048]{1,0:T(8,128)(2,1)} %get-tuple-element.24.first_ref), channel_id=1, source_target_pairs={{0,8},{1,9},{2,10},{3,11},{4,12},{5,13},{6,14},{7,15},{8,0},{9,1},... | collective-permute-start | bytes 1572872 | tf_op jit(solution)/shard_map/ppermute | solution.py:180
  57.6 44.8 %collective-permute-start.13 = (bf16[128,2048]{1,0:T(8,128)(2,1)}, bf16[128,2048]{1,0:T(8,128)(2,1)S(1)}, u32[]{:S(2)}, u32[]{:S(2)}) collective-permute-start(bf16[128,2048]{1,0:T(8,128)(2,1)} %get-tuple-element.24.first_ref), channel_id=1, source_target_pairs={{0,2},{1,3},{2,0},{3,1},{4,6},{5,7},{6,4},{7,5},{8,10},{9,11},{10,... | collective-permute-start | bytes 1572872 | tf_op jit(solution)/shard_map/ppermute | solution.py:180
  72.4 34.1 %collective-permute-start.2 = (bf16[128,2048]{1,0:T(8,128)(2,1)S(1)}, bf16[128,2048]{1,0:T(8,128)(2,1)S(1)}, u32[]{:S(2)}, u32[]{:S(2)}) collective-permute-start(bf16[128,2048]{1,0:T(8,128)(2,1)S(1)} %collective-permute-done.1.first_ref), channel_id=1, source_target_pairs={{0,2},{1,3},{2,0},{3,1},{4,6},{5,7},{6,4},{7,5},{8,10},{9,11},{10,... | collective-permute-start | bytes 1572872 | tf_op jit(solution)/shard_map/ppermute | solution.py:180
  74.7 3.0 %copy-start.3 = (bf16[128,2048]{1,0:T(8,128)(2,1)S(1)}, bf16[128,2048]{1,0:T(8,128)(2,1)}, u32[]{:S(2)}) copy-start(bf16[128,2048]{1,0:T(8,128)(2,1)} %get-tuple-element.24.first_ref) | copy-start | bytes 1572868
  74.7 27.8 %copy-start = (bf16[8,144,128]{2,1,0:T(8,128)(2,1)S(1)}, bf16[8,144,128]{2,1,0:T(8,128)(2,1)}, u32[]{:S(2)}) copy-start(bf16[8,144,128]{2,1,0:T(8,128)(2,1)} %all_to_all.11.back_ref) | copy-start | bytes 884740
  74.7 27.8 %copy-start.4 = (bf16[2048,2]{0,1:T(2,128)(2,1)S(1)}, bf16[2048,2]{0,1:T(2,128)(2,1)}, u32[]{:S(2)}) copy-start(bf16[2048,2]{0,1:T(2,128)(2,1)} %param.20) | copy-start | bytes 24580
  77.7 43.2 %collective-permute-start.14 = (bf16[128,2048]{1,0:T(8,128)(2,1)S(1)}, bf16[128,2048]{1,0:T(8,128)(2,1)S(1)}, u32[]{:S(2)}, u32[]{:S(2)}) collective-permute-start(bf16[128,2048]{1,0:T(8,128)(2,1)S(1)} %copy-done.3), channel_id=1, source_target_pairs={{0,4},{1,5},{2,6},{3,7},{4,0},{5,1},{6,2},{7,3},{8,12},{9,13},{10,... | collective-permute-start | bytes 1572872 | tf_op jit(solution)/shard_map/ppermute | solution.py:180
  101.7 14.8 %collective-permute-start.10 = (bf16[128,2048]{1,0:T(8,128)(2,1)S(1)}, bf16[128,2048]{1,0:T(8,128)(2,1)S(1)}, u32[]{:S(2)}, u32[]{:S(2)}) collective-permute-start(bf16[128,2048]{1,0:T(8,128)(2,1)S(1)} %collective-permute-done.9.first_ref), channel_id=1, source_target_pairs={{0,2},{1,3},{2,0},{3,1},{4,6},{5,7},{6,4},{7,5},{8,10},{9,11},{10,... | collective-permute-start | bytes 1572872 | tf_op jit(solution)/shard_map/ppermute | solution.py:180
  102.5 21.6 %collective-permute-start.15 = (bf16[128,2048]{1,0:T(8,128)(2,1)S(1)}, bf16[128,2048]{1,0:T(8,128)(2,1)S(1)}, u32[]{:S(2)}, u32[]{:S(2)}) collective-permute-start(bf16[128,2048]{1,0:T(8,128)(2,1)S(1)} %collective-permute-done.13.second_ref), channel_id=1, source_target_pairs={{0,4},{1,5},{2,6},{3,7},{4,0},{5,1},{6,2},{7,3},{8,12},{9,13},{10,... | collective-permute-start | bytes 1572872 | tf_op jit(solution)/shard_map/ppermute | solution.py:180
  110.4 20.0 %collective-permute-start.7 = (bf16[128,2048]{1,0:T(8,128)(2,1)S(1)}, bf16[128,2048]{1,0:T(8,128)(2,1)S(1)}, u32[]{:S(2)}, u32[]{:S(2)}) collective-permute-start(bf16[128,2048]{1,0:T(8,128)(2,1)S(1)} %get-tuple-element.34), channel_id=1, source_target_pairs={{0,2},{1,3},{2,0},{3,1},{4,6},{5,7},{6,4},{7,5},{8,10},{9,11},{10,... | collective-permute-start | bytes 1572872 | tf_op jit(solution)/shard_map/ppermute | solution.py:180
  120.5 16.0 %collective-permute-start.11 = (bf16[128,2048]{1,0:T(8,128)(2,1)S(1)}, bf16[128,2048]{1,0:T(8,128)(2,1)S(1)}, u32[]{:S(2)}, u32[]{:S(2)}) collective-permute-start(bf16[128,2048]{1,0:T(8,128)(2,1)S(1)} %get-tuple-element.36), channel_id=1, source_target_pairs={{0,2},{1,3},{2,0},{3,1},{4,6},{5,7},{6,4},{7,5},{8,10},{9,11},{10,... | collective-permute-start | bytes 1572872 | tf_op jit(solution)/shard_map/ppermute | solution.py:180
  128.3 15.6 %collective-permute-start.17 = (bf16[128,2048]{1,0:T(8,128)(2,1)S(1)}, bf16[128,2048]{1,0:T(8,128)(2,1)S(1)}, u32[]{:S(2)}, u32[]{:S(2)}) collective-permute-start(bf16[128,2048]{1,0:T(8,128)(2,1)S(1)} %get-tuple-element.40), channel_id=1, source_target_pairs={{0,4},{1,5},{2,6},{3,7},{4,0},{5,1},{6,2},{7,3},{8,12},{9,13},{10,... | collective-permute-start | bytes 1572872 | tf_op jit(solution)/shard_map/ppermute | solution.py:180
  128.4 47.0 %collective-permute-start.16 = (bf16[128,2048]{1,0:T(8,128)(2,1)S(1)}, bf16[128,2048]{1,0:T(8,128)(2,1)S(1)}, u32[]{:S(2)}, u32[]{:S(2)}) collective-permute-start(bf16[128,2048]{1,0:T(8,128)(2,1)S(1)} %get-tuple-element.38), channel_id=1, source_target_pairs={{0,4},{1,5},{2,6},{3,7},{4,0},{5,1},{6,2},{7,3},{8,12},{9,13},{10,... | collective-permute-start | bytes 1572872 | tf_op jit(solution)/shard_map/ppermute | solution.py:180
  130.5 44.9 %collective-permute-start.8 = (bf16[128,2048]{1,0:T(8,128)(2,1)S(1)}, bf16[128,2048]{1,0:T(8,128)(2,1)S(1)}, u32[]{:S(2)}, u32[]{:S(2)}) collective-permute-start(bf16[128,2048]{1,0:T(8,128)(2,1)S(1)} %add_convert_fusion.3), channel_id=1, source_target_pairs={{0,12},{1,13},{2,14},{3,15},{4,8},{5,9},{6,10},{7,11},{8,4},{9,5},... | collective-permute-start | bytes 1572872 | tf_op jit(solution)/shard_map/ppermute | solution.py:180
  136.6 40.8 %collective-permute-start.12 = (bf16[128,2048]{1,0:T(8,128)(2,1)S(1)}, bf16[128,2048]{1,0:T(8,128)(2,1)S(1)}, u32[]{:S(2)}, u32[]{:S(2)}) collective-permute-start(bf16[128,2048]{1,0:T(8,128)(2,1)S(1)} %add_convert_fusion.2), channel_id=1, source_target_pairs={{0,8},{1,9},{2,10},{3,11},{4,12},{5,13},{6,14},{7,15},{8,0},{9,1},... | collective-permute-start | bytes 1572872 | tf_op jit(solution)/shard_map/ppermute | solution.py:180
  144.0 33.4 %collective-permute-start.18 = (bf16[128,2048]{1,0:T(8,128)(2,1)S(1)}, bf16[128,2048]{1,0:T(8,128)(2,1)S(1)}, u32[]{:S(2)}, u32[]{:S(2)}) collective-permute-start(bf16[128,2048]{1,0:T(8,128)(2,1)S(1)} %add_convert_fusion.1), channel_id=1, source_target_pairs={{0,2},{1,3},{2,0},{3,1},{4,6},{5,7},{6,4},{7,5},{8,10},{9,11},{10,... | collective-permute-start | bytes 1572872 | tf_op jit(solution)/shard_map/ppermute | solution.py:180

commit v3 on v2

--- a/solution.py
+++ b/solution.py
@@ -216,24 +216,31 @@
     copy_all(zip(refs[:count], refs[count : 2 * count]), refs[-1])
 
 
-def load(*arrays):
+def load(mib, *arrays):
     outs = [pltpu.VMEM(array.shape, array.dtype) for array in arrays]
     count = len(arrays)
-    return call(load_kernel, outs, [HBM] * count, 0, 36, *arrays, copies=count)
-
-
-def pack_kernel(query_ref, key_ref, value_ref, out_ref, sems):
-    copy_all(
-        [
-            (ref.at[:, pl.ds(head * DH, DH)], out_ref.at[head, :, pl.ds(at * DH, DH)])
-            for at, ref in enumerate((query_ref, key_ref, value_ref))
-            for head in range(out_ref.shape[0])
-        ],
-        sems,
-    )
-
-
-def attention_kernel(index_ref, own_ref, other_ref, ids_ref, out_ref):
+    return call(load_kernel, outs, [HBM] * count, 0, mib, *arrays, copies=count)
+
+
+def pack_kernel(index_ref, query_ref, key_ref, value_ref, *refs):
+    pairs = []
+    for at, out_ref in enumerate(refs[:-1]):
+        head = (index_ref[0] ^ 2 * at) >> 1
+        columns = pl.ds(pl.multiple_of(head * DH, DH), DH)
+        for part, ref in enumerate((query_ref, key_ref, value_ref)):
+            pairs.append((ref.at[:, columns], out_ref.at[:, pl.ds(part * DH, DH)]))
+    copy_all(pairs, refs[-1])
+
+
+def arrange_kernel(index_ref, *refs):
+    query_ref, pair_ref = refs[-2:]
+    for at, ref in enumerate(refs[:-2]):
+        place = (index_ref[0] ^ 2 * at) >> 1
+        query_ref[place] = ref[:, :DH]
+        pair_ref[place] = ref[:, DH:]
+
+
+def attention_kernel(index_ref, query_ref, own_ref, other_ref, ids_ref, out_ref):
     core = index_ref[0] & 1
     blocks, rows, _ = own_ref.shape
     row_at = lax.broadcasted_iota(jnp.int32, (rows, rows), 0)
@@ -245,13 +252,13 @@
         ids_ref[...].astype(jnp.float32), (out_ref.shape[1] - rows, rows)
     ).astype(jnp.bfloat16)
     for block in range(blocks):
-        query = own_ref[block, :, :DH]
+        query = query_ref[block]
         scores = []
         for ref, last_visible in ((own_ref, causal), (other_ref, also)):
             for at in range(block + 1):
                 score = lax.dot_general(
                     query,
-                    ref[at, :, DH : 2 * DH],
+                    ref[at, :, :DH],
                     contract,
                     preferred_element_type=jnp.float32,
                 ) * DH ** (-0.5)
@@ -270,7 +277,7 @@
             ref = own_ref if at <= block else other_ref
             numer = numer + jnp.dot(
                 weights.astype(jnp.bfloat16),
-                ref[at % (block + 1), :, 2 * DH :],
+                ref[at % (block + 1), :, DH:],
                 preferred_element_type=jnp.float32,
             )
         totals = jnp.sum(summed, axis=1, keepdims=True)
@@ -394,31 +401,42 @@
         axis_index_groups=[list(range(parity, ctx_count, 2)) for parity in range(2)],
     )
     shape = jax.ShapeDtypeStruct
-    (packed,) = call(
+    packed = call(
         pack_kernel,
-        [shape((heads, rows, 3 * DH), jnp.bfloat16)],
-        [HBM] * 3,
+        [shape((rows, 3 * DH), jnp.bfloat16)] * heads,
+        [SMEM] + [HBM] * 3,
         0,
         62,
+        index,
         queries,
         keys,
         values,
         copies=3 * heads,
     )
-    own = exchange(packed)
+    blocks = [packed[0]] + [swap(packed[at], 2 * at) for at in range(1, heads)]
+    query, own = call(
+        arrange_kernel,
+        [shape((heads, rows, DH), jnp.bfloat16), shape((heads, rows, 2 * DH), jnp.bfloat16)],
+        [SMEM] + [VMEM] * heads,
+        0,
+        8,
+        index,
+        *blocks,
+    )
     other = swap(own, 1)
     weights_own = (up_proj, expert_in[0], down_proj, expert_out[0])
     weights_other = [swap(array, 1) for array in weights_own]
-    weights_own = load(*weights_own)
-    weights_other = load(*weights_other)
+    weights_own = load(51, *weights_own)
+    weights_other = load(44, *weights_other)
     weights = tuple(w for pair in zip(weights_own, weights_other) for w in pair)
     (out,) = call(
         attention_kernel,
         [shape((heads, rows + 16, DH), jnp.bfloat16)],
-        [SMEM] + [VMEM] * 3,
+        [SMEM] + [VMEM] * 4,
         10**9,
         12,
         index,
+        query,
         own,
         other,
         expert_ids.reshape(1, rows),

time: 179 us -> 179 us (level)
  blocking collectives: 41.6 us -> 16.4 us
  waiting for transfers between devices: 68.3 us -> 90.7 us
    all_to_all x1 -> x0, blocking collectives: 27.5 us -> none  [body_by_pairs(): own = exchange(packed)]
    ppermute x19 -> x26, waiting for transfers between devices: 68.3 us -> 90.7 us  [swap(): lax.ppermute(array, 'ctx', [(i, i ^ mask) for i in range(lax.axis_size('c...]
    all_to_all x1, blocking collectives: 14.1 us -> 16.4 us  [body_by_pairs(): back = exchange(out)]
    ppermute x19 -> x26, starting transfers between devices: 34.8 us -> 35.9 us  [swap(): lax.ppermute(array, 'ctx', [(i, i ^ mask) for i in range(lax.axis_size('c...]
    pallas_call x9 -> x10, Pallas kernels: 32.1 us -> 32.1 us  [call(): pl.pallas_call(kernel, out_shape=outs, in_specs=specs, out_specs=[VMEM] *...]
  transfers between devices with their start and end apart: 19 -> 26, of which waited for: 9 -> 11; matrix products, arithmetic and copies ran while one was open for 0% -> 0% of each run, Pallas kernels for 17% -> 17%
where the time goes in v3:
time: 179 us
  waiting for transfers between devices  90.7 us (51%)
  starting transfers between devices  35.9 us (20%)
  Pallas kernels  32.1 us (18%)
  blocking collectives  16.4 us (9%)
    ppermute x26, waiting for transfers between devices, swap(): lax.ppermute(array, 'ctx', [(i, i ^ mask) for i in range(lax.axis_size('c...  90.7 us
    ppermute x26, starting transfers between devices, swap(): lax.ppermute(array, 'ctx', [(i, i ^ mask) for i in range(lax.axis_size('c...  35.9 us
    pallas_call x10, Pallas kernels, call(): pl.pallas_call(kernel, out_shape=outs, in_specs=specs, out_specs=[VMEM] *...  32.1 us
    all_to_all x1, blocking collectives, body_by_pairs(): back = exchange(out)  16.4 us
  transfers between devices with their start and end apart: 26, of which 11 were waited for; matrix products, arithmetic and copies ran while one was open for 0% of the time, Pallas kernels for 17%

profile of v3, /device:TPU:0, one launch (start us, length us, event | category | flops | bytes accessed | tf_op | source)
XLA Modules:
  0.0 178.6 jit_solution(1617335913246722163)
XLA Ops:
  0.0 2.2 %shard_map.118 = (bf16[128,384]{1,0:T(8,128)(2,1)}, bf16[128,384]{1,0:T(8,128)(2,1)}, bf16[128,384]{1,0:T(8,128)(2,1)}, bf16[128,384]{1,0:T(8,128)(2,1)}, bf16[1...) custom-call(s32[1]{0:T(128)} %bitcast.index_ref, ...), custom_call_target="tpu_custom_call" | custom-call | bytes 786436 | tf_op jit(solution)/shard_map/pallas_call | solution.py:191
  2.2 3.1 %collective-permute-start = (bf16[128,384]{1,0:T(8,128)(2,1)}, bf16[128,384]{1,0:T(8,128)(2,1)S(1)}, u32[]{:S(2)}, u32[]{:S(2)}) collective-permute-start(bf16[128,384]{1,0:T(8,128)(2,1)} %get-tuple-element.34), channel_id=1, source_target_pairs={{0,2},{1,3},{2,0},{3,1},{4,6},{5,7},{6,4},{7,5},{8,10},{9,11},{10,... | collective-permute-start | bytes 294920 | tf_op jit(solution)/shard_map/ppermute | solution.py:180
  5.2 1.6 collective-permute-start.1
  6.8 3.0 %collective-permute-start.3 = (bf16[128,384]{1,0:T(8,128)(2,1)}, bf16[128,384]{1,0:T(8,128)(2,1)S(1)}, u32[]{:S(2)}, u32[]{:S(2)}) collective-permute-start(bf16[128,384]{1,0:T(8,128)(2,1)} %get-tuple-element.37), channel_id=1, source_target_pairs={{0,8},{1,9},{2,10},{3,11},{4,12},{5,13},{6,14},{7,15},{8,0},{9,1},... | collective-permute-start | bytes 294920 | tf_op jit(solution)/shard_map/ppermute | solution.py:180
  10.3 2.7 %collective-permute-done.1.refs_2_ = bf16[128,384]{1,0:T(8,128)(2,1)S(1)} collective-permute-done((bf16[128,384]{1,0:T(8,128)(2,1)}, bf16[128,384]{1,0:T(8,128)(2,1)S(1)}, u32[]{:S(2)}, u32[]{:S(2)}) %collective-permute-start.1) | collective-permute-done | bytes 98336 | tf_op jit(solution)/shard_map/ppermute | solution.py:180
  13.3 3.0 %collective-permute-start.5 = (bf16[128,384]{1,0:T(8,128)(2,1)}, bf16[128,384]{1,0:T(8,128)(2,1)S(1)}, u32[]{:S(2)}, u32[]{:S(2)}) collective-permute-start(bf16[128,384]{1,0:T(8,128)(2,1)} %get-tuple-element.39), channel_id=1, source_target_pairs={{0,12},{1,13},{2,14},{3,15},{4,8},{5,9},{6,10},{7,11},{8,4},{9,5},... | collective-permute-start | bytes 294920 | tf_op jit(solution)/shard_map/ppermute | solution.py:180
  16.3 8.5 %collective-permute-start.6 = (bf16[128,384]{1,0:T(8,128)(2,1)}, bf16[128,384]{1,0:T(8,128)(2,1)S(1)}, u32[]{:S(2)}, u32[]{:S(2)}) collective-permute-start(bf16[128,384]{1,0:T(8,128)(2,1)} %get-tuple-element.40), channel_id=1, source_target_pairs={{0,14},{1,15},{2,12},{3,13},{4,10},{5,11},{6,8},{7,9},{8,6},{9,7},... | collective-permute-start | bytes 294920 | tf_op jit(solution)/shard_map/ppermute | solution.py:180
  24.8 2.9 %collective-permute-done.6.refs_7_ = bf16[128,384]{1,0:T(8,128)(2,1)S(1)} collective-permute-done((bf16[128,384]{1,0:T(8,128)(2,1)}, bf16[128,384]{1,0:T(8,128)(2,1)S(1)}, u32[]{:S(2)}, u32[]{:S(2)}) %collective-permute-start.6) | collective-permute-done | bytes 98336 | tf_op jit(solution)/shard_map/ppermute | solution.py:180
  29.3 1.3 collective-permute-done.7.other_ref
  31.3 4.1 %shard_map.120 = bf16[8,144,128]{2,1,0:T(8,128)(2,1)S(1)} custom-call(s32[1]{0:T(128)} %bitcast.index_ref, bf16[8,128,128]{2,1,0:T(8,128)(2,1)S(1)} %get-tuple-element.41.query_ref, bf16[8,128,256]{2,1,0:T(8,128)(2,1)S(1)} %get-tuple-element.42.own_ref, bf16[8,128,256]{2,1,0:T(8,128)(2,1)S(1)} %collective-permute-done.7.other_ref, s32[1,128]{1,0:T(1,128)S(1)} %bitcast.10), custom_call_target="tpu_custom_call" | custom-call | flops 1000000000 | bytes 1311236 | tf_op jit(solution)/shard_map/pallas_call | solution.py:191
  35.4 16.4 %all_to_all.5.back_ref = bf16[8,144,128]{2,1,0:T(8,128)(2,1)} all-to-all(bf16[8,144,128]{2,1,0:T(8,128)(2,1)S(1)} %shard_map.120), channel_id=1, replica_groups={{0,2,4,6,8,10,12,14},{1,3,5,7,9,11,13,15},{16,18,20,22,24,26,28,30},{17..., dimensions={0} | all-to-all | bytes 589824 | tf_op jit(solution)/shard_map/all_to_all | solution.py:444
  51.8 4.7 %shard_map.121 = (f32[128,2048]{1,0:T(8,128)S(1)}, bf16[128,2048]{1,0:T(8,128)(2,1)}) custom-call(bf16[8,144,128]{2,1,0:T(8,128)(2,1)} %all_to_all.5.back_ref, bf16[1024,2048]{1,0:T(8,128)(2,1)} %weight_ref.1, bf16[128,2048]{1,0:T(8,128)(2,1)} %resid_ref.1, f32[1,2048]{1,0:T(1,128)} %bitcast.15), custom_call_target="tpu_custom_call" | custom-call | flops 536870912 | bytes 5021696 | tf_op jit(solution)/shard_map/pallas_call | solution.py:191
  56.5 1.5 collective-permute-start.8
  59.2 14.2 %collective-permute-done.8.first_ref = bf16[128,2048]{1,0:T(8,128)(2,1)S(1)} collective-permute-done((bf16[128,2048]{1,0:T(8,128)(2,1)}, bf16[128,2048]{1,0:T(8,128)(2,1)S(1)}, u32[]{:S(2)}, u32[]{:S(2)}) %collective-permute-start.8) | collective-permute-done | bytes 524320 | tf_op jit(solution)/shard_map/ppermute | solution.py:180
  74.1 2.9 %shard_map.122 = (bf16[2048,256]{1,0:T(8,128)(2,1)S(1)}, bf16[2048,512]{1,0:T(8,128)(2,1)S(1)}, bf16[2048,256]{1,0:T(8,128)(2,1)S(1)}, bf16[512,2048]{1,0:T(8,128)(2,1)S(1)}) custom-call(bf16[2048,256]{1,0:T(8,128)(2,1)} %refs_0_.1, bf16[2048,512]{1,0:T(8,128)(2,1)} %bitcast.12, bf16[2048,256]{1,0:T(8,128)(2,1)} %refs_2_.1, bf16[512,2048]{1,0:T(8,128)(2,1)} %bitcast.14), custom_call_target="tpu_custom_call" | custom-call | bytes 6291456 | tf_op jit(solution)/shard_map/pallas_call | solution.py:191
  77.1 25.6 %collective-permute-done.16.first_ref = bf16[128,2048]{1,0:T(8,128)(2,1)S(1)} collective-permute-done((bf16[128,2048]{1,0:T(8,128)(2,1)}, bf16[128,2048]{1,0:T(8,128)(2,1)S(1)}, u32[]{:S(2)}, u32[]{:S(2)}) %collective-permute-start.16) | collective-permute-done | bytes 524320 | tf_op jit(solution)/shard_map/ppermute | solution.py:180
  103.5 2.0 %collective-permute-start.22 = (bf16[128,2048]{1,0:T(8,128)(2,1)S(1)}, bf16[128,2048]{1,0:T(8,128)(2,1)S(1)}, u32[]{:S(2)}, u32[]{:S(2)}) collective-permute-start(bf16[128,2048]{1,0:T(8,128)(2,1)S(1)} %collective-permute-done.20.second_ref), channel_id=1, source_target_pairs={{0,4},{1,5},{2,6},{3,7},{4,0},{5,1},{6,2},{7,3},{8,12},{9,13},{10,... | collective-permute-start | bytes 1572872 | tf_op jit(solution)/shard_map/ppermute | solution.py:180
  105.5 2.4 %shard_map.123 = (bf16[2048,256]{1,0:T(8,128)(2,1)S(1)}, bf16[2048,512]{1,0:T(8,128)(2,1)S(1)}, bf16[2048,256]{1,0:T(8,128)(2,1)S(1)}, bf16[512,2048]{1,0:T(8,128)(2,1)S(1)}) custom-call(bf16[2048,256]{1,0:T(8,128)(2,1)S(1)} %collective-permute-done.10.refs_0_, bf16[2048,512]{1,0:T(8,128)(2,1)} %collective-permute-done.11.refs_1_, ...), custom_call_target="tpu_custom_call" | custom-call | bytes 6291456 | tf_op jit(solution)/shard_map/pallas_call | solution.py:191
  107.9 3.9 %shard_map.126 = (bf16[128,2048]{1,0:T(8,128)(2,1)S(1)}, bf16[128,2048]{1,0:T(8,128)(2,1)S(1)}) custom-call(s32[1]{0:T(128)} %bitcast.index_ref, bf16[128,2048]{1,0:T(8,128)(2,1)S(1)} %copy-done.1, bf16[128,2048]{1,0:T(8,128)(2,1)S(1)} %collective-permute-done.20.second_ref, bf16[8,144,128]{2,1,0:T(8,128)(2,1)S(1)} %copy-done, bf16[2,2048]{1,0:T(2,128)(2,1)S(1)} %bitcast.6, ...), custom_call_target="tpu_custom_call" | custom-call | flops 3221225472 | bytes 13934596 | tf_op jit(solution)/shard_map/pallas_call | solution.py:191
  111.8 4.0 %shard_map.124 = (bf16[128,2048]{1,0:T(8,128)(2,1)S(1)}, bf16[128,2048]{1,0:T(8,128)(2,1)S(1)}) custom-call(s32[1]{0:T(128)} %bitcast.index_ref, bf16[128,2048]{1,0:T(8,128)(2,1)S(1)} %collective-permute-done.8.first_ref, bf16[128,2048]{1,0:T(8,128)(2,1)S(1)} %collective-permute-done.9.second_ref, bf16[8,144,128]{2,1,0:T(8,128)(2,1)S(1)} %copy-done, ...), custom_call_target="tpu_custom_call" | custom-call | flops 3221225472 | bytes 13934596 | tf_op jit(solution)/shard_map/pallas_call | solution.py:191
  115.8 1.3 collective-permute-start.14
  117.2 3.9 %shard_map.125 = (bf16[128,2048]{1,0:T(8,128)(2,1)S(1)}, bf16[128,2048]{1,0:T(8,128)(2,1)S(1)}) custom-call(s32[1]{0:T(128)} %bitcast.index_ref, bf16[128,2048]{1,0:T(8,128)(2,1)S(1)} %collective-permute-done.16.first_ref, bf16[128,2048]{1,0:T(8,128)(2,1)S(1)} %collective-permute-done.17.second_ref, bf16[8,144,128]{2,1,0:T(8,128)(2,1)S(1)} %copy-done, ...), custom_call_target="tpu_custom_call" | custom-call | flops 3221225472 | bytes 13934596 | tf_op jit(solution)/shard_map/pallas_call | solution.py:191
  121.9 4.3 %collective-permute-done.22.second_ref = bf16[128,2048]{1,0:T(8,128)(2,1)S(1)} collective-permute-done((bf16[128,2048]{1,0:T(8,128)(2,1)S(1)}, bf16[128,2048]{1,0:T(8,128)(2,1)S(1)}, u32[]{:S(2)}, u32[]{:S(2)}) %collective-permute-start.22) | collective-permute-done | bytes 524320 | tf_op jit(solution)/shard_map/ppermute | solution.py:180
  126.2 3.9 %shard_map.127 = (bf16[128,2048]{1,0:T(8,128)(2,1)S(1)}, bf16[128,2048]{1,0:T(8,128)(2,1)S(1)}) custom-call(s32[1]{0:T(128)} %bitcast.index_ref, bf16[128,2048]{1,0:T(8,128)(2,1)S(1)} %collective-permute-done.21.first_ref, bf16[128,2048]{1,0:T(8,128)(2,1)S(1)} %collective-permute-done.22.second_ref, bf16[8,144,128]{2,1,0:T(8,128)(2,1)S(1)} %copy-done, ...), custom_call_target="tpu_custom_call" | custom-call | flops 3221225472 | bytes 13934596 | tf_op jit(solution)/shard_map/pallas_call | solution.py:191
  130.5 1.7 collective-permute-start.23
  132.4 2.8 %collective-permute-start.15 = (bf16[128,2048]{1,0:T(8,128)(2,1)S(1)}, bf16[128,2048]{1,0:T(8,128)(2,1)S(1)}, u32[]{:S(2)}, u32[]{:S(2)}) collective-permute-start(bf16[128,2048]{1,0:T(8,128)(2,1)S(1)} %add_convert_fusion.3), channel_id=1, source_target_pairs={{0,12},{1,13},{2,14},{3,15},{4,8},{5,9},{6,10},{7,11},{8,4},{9,5},... | collective-permute-start | bytes 1572872 | tf_op jit(solution)/shard_map/ppermute | solution.py:180
  135.2 3.4 %collective-permute-done.18 = bf16[128,2048]{1,0:T(8,128)(2,1)S(1)} collective-permute-done((bf16[128,2048]{1,0:T(8,128)(2,1)S(1)}, bf16[128,2048]{1,0:T(8,128)(2,1)S(1)}, u32[]{:S(2)}, u32[]{:S(2)}) %collective-permute-start.18) | collective-permute-done | bytes 524320 | tf_op jit(solution)/shard_map/ppermute | solution.py:180
  138.7 2.0 %collective-permute-start.19 = (bf16[128,2048]{1,0:T(8,128)(2,1)S(1)}, bf16[128,2048]{1,0:T(8,128)(2,1)S(1)}, u32[]{:S(2)}, u32[]{:S(2)}) collective-permute-start(bf16[128,2048]{1,0:T(8,128)(2,1)S(1)} %add_convert_fusion.2), channel_id=1, source_target_pairs={{0,8},{1,9},{2,10},{3,11},{4,12},{5,13},{6,14},{7,15},{8,0},{9,1},... | collective-permute-start | bytes 1572872 | tf_op jit(solution)/shard_map/ppermute | solution.py:180
  140.7 24.9 %collective-permute-done.24 = bf16[128,2048]{1,0:T(8,128)(2,1)S(1)} collective-permute-done((bf16[128,2048]{1,0:T(8,128)(2,1)S(1)}, bf16[128,2048]{1,0:T(8,128)(2,1)S(1)}, u32[]{:S(2)}, u32[]{:S(2)}) %collective-permute-start.24) | collective-permute-done | bytes 524320 | tf_op jit(solution)/shard_map/ppermute | solution.py:180
  166.2 8.8 %collective-permute-done.23 = bf16[128,2048]{1,0:T(8,128)(2,1)S(1)} collective-permute-done((bf16[128,2048]{1,0:T(8,128)(2,1)S(1)}, bf16[128,2048]{1,0:T(8,128)(2,1)S(1)}, u32[]{:S(2)}, u32[]{:S(2)}) %collective-permute-start.23) | collective-permute-done | bytes 524320 | tf_op jit(solution)/shard_map/ppermute | solution.py:180
  175.0 2.3 %collective-permute-done.19 = bf16[128,2048]{1,0:T(8,128)(2,1)S(1)} collective-permute-done((bf16[128,2048]{1,0:T(8,128)(2,1)S(1)}, bf16[128,2048]{1,0:T(8,128)(2,1)S(1)}, u32[]{:S(2)}, u32[]{:S(2)}) %collective-permute-start.19) | collective-permute-done | bytes 524320 | tf_op jit(solution)/shard_map/ppermute | solution.py:180
  177.3 1.3 add_convert_fusion
  (45 shorter events, 7.9 us)
Async XLA Ops:
  2.2 7.6 %collective-permute-start = (bf16[128,384]{1,0:T(8,128)(2,1)}, bf16[128,384]{1,0:T(8,128)(2,1)S(1)}, u32[]{:S(2)}, u32[]{:S(2)}) collective-permute-start(bf16[128,384]{1,0:T(8,128)(2,1)} %get-tuple-element.34), channel_id=1, source_target_pairs={{0,2},{1,3},{2,0},{3,1},{4,6},{5,7},{6,4},{7,5},{8,10},{9,11},{10,... | collective-permute-start | bytes 294920 | tf_op jit(solution)/shard_map/ppermute | solution.py:180
  5.2 7.8 %collective-permute-start.1 = (bf16[128,384]{1,0:T(8,128)(2,1)}, bf16[128,384]{1,0:T(8,128)(2,1)S(1)}, u32[]{:S(2)}, u32[]{:S(2)}) collective-permute-start(bf16[128,384]{1,0:T(8,128)(2,1)} %get-tuple-element.35), channel_id=1, source_target_pairs={{0,4},{1,5},{2,6},{3,7},{4,0},{5,1},{6,2},{7,3},{8,12},{9,13},{10,... | collective-permute-start | bytes 294920 | tf_op jit(solution)/shard_map/ppermute | solution.py:180
  6.8 6.5 %collective-permute-start.2 = (bf16[128,384]{1,0:T(8,128)(2,1)}, bf16[128,384]{1,0:T(8,128)(2,1)S(1)}, u32[]{:S(2)}, u32[]{:S(2)}) collective-permute-start(bf16[128,384]{1,0:T(8,128)(2,1)} %get-tuple-element.36), channel_id=1, source_target_pairs={{0,6},{1,7},{2,4},{3,5},{4,2},{5,3},{6,0},{7,1},{8,14},{9,15},{10,... | collective-permute-start | bytes 294920 | tf_op jit(solution)/shard_map/ppermute | solution.py:180
  6.8 9.5 %collective-permute-start.3 = (bf16[128,384]{1,0:T(8,128)(2,1)}, bf16[128,384]{1,0:T(8,128)(2,1)S(1)}, u32[]{:S(2)}, u32[]{:S(2)}) collective-permute-start(bf16[128,384]{1,0:T(8,128)(2,1)} %get-tuple-element.37), channel_id=1, source_target_pairs={{0,8},{1,9},{2,10},{3,11},{4,12},{5,13},{6,14},{7,15},{8,0},{9,1},... | collective-permute-start | bytes 294920 | tf_op jit(solution)/shard_map/ppermute | solution.py:180
  9.8 93.7 %collective-permute-start.11 = (bf16[2048,512]{1,0:T(8,128)(2,1)}, bf16[2048,512]{1,0:T(8,128)(2,1)}, u32[]{:S(2)}, u32[]{:S(2)}) collective-permute-start(bf16[2048,512]{1,0:T(8,128)(2,1)} %bitcast.11), channel_id=1, source_target_pairs={{0,1},{1,0},{2,3},{3,2},{4,5},{5,4},{6,7},{7,6},{8,9},{9,8},{10,11... | collective-permute-start | bytes 6291464 | tf_op jit(solution)/shard_map/ppermute | solution.py:180
  9.8 95.6 %collective-permute-start.13 = (bf16[512,2048]{1,0:T(8,128)(2,1)}, bf16[512,2048]{1,0:T(8,128)(2,1)}, u32[]{:S(2)}, u32[]{:S(2)}) collective-permute-start(bf16[512,2048]{1,0:T(8,128)(2,1)} %bitcast.13), channel_id=1, source_target_pairs={{0,1},{1,0},{2,3},{3,2},{4,5},{5,4},{6,7},{7,6},{8,9},{9,8},{10,11... | collective-permute-start | bytes 6291464 | tf_op jit(solution)/shard_map/ppermute | solution.py:180
  13.1 11.7 %collective-permute-start.4 = (bf16[128,384]{1,0:T(8,128)(2,1)}, bf16[128,384]{1,0:T(8,128)(2,1)S(1)}, u32[]{:S(2)}, u32[]{:S(2)}) collective-permute-start(bf16[128,384]{1,0:T(8,128)(2,1)} %get-tuple-element.38), channel_id=1, source_target_pairs={{0,10},{1,11},{2,8},{3,9},{4,14},{5,15},{6,12},{7,13},{8,2},{9,3},... | collective-permute-start | bytes 294920 | tf_op jit(solution)/shard_map/ppermute | solution.py:180
  13.3 11.5 %collective-permute-start.5 = (bf16[128,384]{1,0:T(8,128)(2,1)}, bf16[128,384]{1,0:T(8,128)(2,1)S(1)}, u32[]{:S(2)}, u32[]{:S(2)}) collective-permute-start(bf16[128,384]{1,0:T(8,128)(2,1)} %get-tuple-element.39), channel_id=1, source_target_pairs={{0,12},{1,13},{2,14},{3,15},{4,8},{5,9},{6,10},{7,11},{8,4},{9,5},... | collective-permute-start | bytes 294920 | tf_op jit(solution)/shard_map/ppermute | solution.py:180
  16.3 11.4 %collective-permute-start.6 = (bf16[128,384]{1,0:T(8,128)(2,1)}, bf16[128,384]{1,0:T(8,128)(2,1)S(1)}, u32[]{:S(2)}, u32[]{:S(2)}) collective-permute-start(bf16[128,384]{1,0:T(8,128)(2,1)} %get-tuple-element.40), channel_id=1, source_target_pairs={{0,14},{1,15},{2,12},{3,13},{4,10},{5,11},{6,8},{7,9},{8,6},{9,7},... | collective-permute-start | bytes 294920 | tf_op jit(solution)/shard_map/ppermute | solution.py:180
  27.7 0.9 copy-start.3
  28.7 2.0 %collective-permute-start.7 = (bf16[8,128,256]{2,1,0:T(8,128)(2,1)S(1)}, bf16[8,128,256]{2,1,0:T(8,128)(2,1)S(1)}, u32[]{:S(2)}, u32[]{:S(2)}) collective-permute-start(bf16[8,128,256]{2,1,0:T(8,128)(2,1)S(1)} %get-tuple-element.42.own_ref), channel_id=1, source_target_pairs={{0,1},{1,0},{2,3},{3,2},{4,5},{5,4},{6,7},{7,6},{8,9},{9,8},{10,11... | collective-permute-start | bytes 1572872 | tf_op jit(solution)/shard_map/ppermute | solution.py:180
  28.7 29.3 %collective-permute-start.10 = (bf16[2048,256]{1,0:T(8,128)(2,1)}, bf16[2048,256]{1,0:T(8,128)(2,1)S(1)}, u32[]{:S(2)}, u32[]{:S(2)}) collective-permute-start(bf16[2048,256]{1,0:T(8,128)(2,1)} %refs_0_.1), channel_id=1, source_target_pairs={{0,1},{1,0},{2,3},{3,2},{4,5},{5,4},{6,7},{7,6},{8,9},{9,8},{10,11... | collective-permute-start | bytes 3145736 | tf_op jit(solution)/shard_map/ppermute | solution.py:180
  29.2 29.5 %collective-permute-start.12 = (bf16[2048,256]{1,0:T(8,128)(2,1)}, bf16[2048,256]{1,0:T(8,128)(2,1)S(1)}, u32[]{:S(2)}, u32[]{:S(2)}) collective-permute-start(bf16[2048,256]{1,0:T(8,128)(2,1)} %refs_2_.1), channel_id=1, source_target_pairs={{0,1},{1,0},{2,3},{3,2},{4,5},{5,4},{6,7},{7,6},{8,9},{9,8},{10,11... | collective-permute-start | bytes 3145736 | tf_op jit(solution)/shard_map/ppermute | solution.py:180
  30.6 0.7 copy-start.4
  56.5 46.2 %copy-start.1 = (bf16[128,2048]{1,0:T(8,128)(2,1)S(1)}, bf16[128,2048]{1,0:T(8,128)(2,1)}, u32[]{:S(2)}) copy-start(bf16[128,2048]{1,0:T(8,128)(2,1)} %get-tuple-element.44.first_ref) | copy-start | bytes 1572868
  56.5 16.9 %collective-permute-start.8 = (bf16[128,2048]{1,0:T(8,128)(2,1)}, bf16[128,2048]{1,0:T(8,128)(2,1)S(1)}, u32[]{:S(2)}, u32[]{:S(2)}) collective-permute-start(bf16[128,2048]{1,0:T(8,128)(2,1)} %get-tuple-element.44.first_ref), channel_id=1, source_target_pairs={{0,12},{1,13},{2,14},{3,15},{4,8},{5,9},{6,10},{7,11},{8,4},{9,5},... | collective-permute-start | bytes 1572872 | tf_op jit(solution)/shard_map/ppermute | solution.py:180
  58.0 44.6 %collective-permute-start.16 = (bf16[128,2048]{1,0:T(8,128)(2,1)}, bf16[128,2048]{1,0:T(8,128)(2,1)S(1)}, u32[]{:S(2)}, u32[]{:S(2)}) collective-permute-start(bf16[128,2048]{1,0:T(8,128)(2,1)} %get-tuple-element.44.first_ref), channel_id=1, source_target_pairs={{0,8},{1,9},{2,10},{3,11},{4,12},{5,13},{6,14},{7,15},{8,0},{9,1},... | collective-permute-start | bytes 1572872 | tf_op jit(solution)/shard_map/ppermute | solution.py:180
  58.7 44.0 %collective-permute-start.20 = (bf16[128,2048]{1,0:T(8,128)(2,1)}, bf16[128,2048]{1,0:T(8,128)(2,1)S(1)}, u32[]{:S(2)}, u32[]{:S(2)}) collective-permute-start(bf16[128,2048]{1,0:T(8,128)(2,1)} %get-tuple-element.44.first_ref), channel_id=1, source_target_pairs={{0,2},{1,3},{2,0},{3,1},{4,6},{5,7},{6,4},{7,5},{8,10},{9,11},{10,... | collective-permute-start | bytes 1572872 | tf_op jit(solution)/shard_map/ppermute | solution.py:180
  73.4 38.4 %collective-permute-start.9 = (bf16[128,2048]{1,0:T(8,128)(2,1)S(1)}, bf16[128,2048]{1,0:T(8,128)(2,1)S(1)}, u32[]{:S(2)}, u32[]{:S(2)}) collective-permute-start(bf16[128,2048]{1,0:T(8,128)(2,1)S(1)} %collective-permute-done.8.first_ref), channel_id=1, source_target_pairs={{0,2},{1,3},{2,0},{3,1},{4,6},{5,7},{6,4},{7,5},{8,10},{9,11},{10,... | collective-permute-start | bytes 1572872 | tf_op jit(solution)/shard_map/ppermute | solution.py:180
  77.0 30.8 %copy-start = (bf16[8,144,128]{2,1,0:T(8,128)(2,1)S(1)}, bf16[8,144,128]{2,1,0:T(8,128)(2,1)}, u32[]{:S(2)}) copy-start(bf16[8,144,128]{2,1,0:T(8,128)(2,1)} %all_to_all.5.back_ref) | copy-start | bytes 884740
  77.1 30.8 %copy-start.2 = (bf16[2048,2]{0,1:T(2,128)(2,1)S(1)}, bf16[2048,2]{0,1:T(2,128)(2,1)}, u32[]{:S(2)}) copy-start(bf16[2048,2]{0,1:T(2,128)(2,1)} %param.20) | copy-start | bytes 24580
  102.7 19.2 %collective-permute-start.21 = (bf16[128,2048]{1,0:T(8,128)(2,1)S(1)}, bf16[128,2048]{1,0:T(8,128)(2,1)S(1)}, u32[]{:S(2)}, u32[]{:S(2)}) collective-permute-start(bf16[128,2048]{1,0:T(8,128)(2,1)S(1)} %copy-done.1), channel_id=1, source_target_pairs={{0,4},{1,5},{2,6},{3,7},{4,0},{5,1},{6,2},{7,3},{8,12},{9,13},{10,... | collective-permute-start | bytes 1572872 | tf_op jit(solution)/shard_map/ppermute | solution.py:180
  102.7 14.5 %collective-permute-start.17 = (bf16[128,2048]{1,0:T(8,128)(2,1)S(1)}, bf16[128,2048]{1,0:T(8,128)(2,1)S(1)}, u32[]{:S(2)}, u32[]{:S(2)}) collective-permute-start(bf16[128,2048]{1,0:T(8,128)(2,1)S(1)} %collective-permute-done.16.first_ref), channel_id=1, source_target_pairs={{0,2},{1,3},{2,0},{3,1},{4,6},{5,7},{6,4},{7,5},{8,10},{9,11},{10,... | collective-permute-start | bytes 1572872 | tf_op jit(solution)/shard_map/ppermute | solution.py:180
  103.5 22.7 %collective-permute-start.22 = (bf16[128,2048]{1,0:T(8,128)(2,1)S(1)}, bf16[128,2048]{1,0:T(8,128)(2,1)S(1)}, u32[]{:S(2)}, u32[]{:S(2)}) collective-permute-start(bf16[128,2048]{1,0:T(8,128)(2,1)S(1)} %collective-permute-done.20.second_ref), channel_id=1, source_target_pairs={{0,4},{1,5},{2,6},{3,7},{4,0},{5,1},{6,2},{7,3},{8,12},{9,13},{10,... | collective-permute-start | bytes 1572872 | tf_op jit(solution)/shard_map/ppermute | solution.py:180
  115.8 16.5 %collective-permute-start.14 = (bf16[128,2048]{1,0:T(8,128)(2,1)S(1)}, bf16[128,2048]{1,0:T(8,128)(2,1)S(1)}, u32[]{:S(2)}, u32[]{:S(2)}) collective-permute-start(bf16[128,2048]{1,0:T(8,128)(2,1)S(1)} %get-tuple-element.54), channel_id=1, source_target_pairs={{0,2},{1,3},{2,0},{3,1},{4,6},{5,7},{6,4},{7,5},{8,10},{9,11},{10,... | collective-permute-start | bytes 1572872 | tf_op jit(solution)/shard_map/ppermute | solution.py:180
  121.1 17.5 %collective-permute-start.18 = (bf16[128,2048]{1,0:T(8,128)(2,1)S(1)}, bf16[128,2048]{1,0:T(8,128)(2,1)S(1)}, u32[]{:S(2)}, u32[]{:S(2)}) collective-permute-start(bf16[128,2048]{1,0:T(8,128)(2,1)S(1)} %get-tuple-element.56), channel_id=1, source_target_pairs={{0,2},{1,3},{2,0},{3,1},{4,6},{5,7},{6,4},{7,5},{8,10},{9,11},{10,... | collective-permute-start | bytes 1572872 | tf_op jit(solution)/shard_map/ppermute | solution.py:180
  130.2 35.4 %collective-permute-start.24 = (bf16[128,2048]{1,0:T(8,128)(2,1)S(1)}, bf16[128,2048]{1,0:T(8,128)(2,1)S(1)}, u32[]{:S(2)}, u32[]{:S(2)}) collective-permute-start(bf16[128,2048]{1,0:T(8,128)(2,1)S(1)} %get-tuple-element.60), channel_id=1, source_target_pairs={{0,4},{1,5},{2,6},{3,7},{4,0},{5,1},{6,2},{7,3},{8,12},{9,13},{10,... | collective-permute-start | bytes 1572872 | tf_op jit(solution)/shard_map/ppermute | solution.py:180
  130.5 44.5 %collective-permute-start.23 = (bf16[128,2048]{1,0:T(8,128)(2,1)S(1)}, bf16[128,2048]{1,0:T(8,128)(2,1)S(1)}, u32[]{:S(2)}, u32[]{:S(2)}) collective-permute-start(bf16[128,2048]{1,0:T(8,128)(2,1)S(1)} %get-tuple-element.58), channel_id=1, source_target_pairs={{0,4},{1,5},{2,6},{3,7},{4,0},{5,1},{6,2},{7,3},{8,12},{9,13},{10,... | collective-permute-start | bytes 1572872 | tf_op jit(solution)/shard_map/ppermute | solution.py:180
  132.4 42.6 %collective-permute-start.15 = (bf16[128,2048]{1,0:T(8,128)(2,1)S(1)}, bf16[128,2048]{1,0:T(8,128)(2,1)S(1)}, u32[]{:S(2)}, u32[]{:S(2)}) collective-permute-start(bf16[128,2048]{1,0:T(8,128)(2,1)S(1)} %add_convert_fusion.3), channel_id=1, source_target_pairs={{0,12},{1,13},{2,14},{3,15},{4,8},{5,9},{6,10},{7,11},{8,4},{9,5},... | collective-permute-start | bytes 1572872 | tf_op jit(solution)/shard_map/ppermute | solution.py:180
  138.7 38.6 %collective-permute-start.19 = (bf16[128,2048]{1,0:T(8,128)(2,1)S(1)}, bf16[128,2048]{1,0:T(8,128)(2,1)S(1)}, u32[]{:S(2)}, u32[]{:S(2)}) collective-permute-start(bf16[128,2048]{1,0:T(8,128)(2,1)S(1)} %add_convert_fusion.2), channel_id=1, source_target_pairs={{0,8},{1,9},{2,10},{3,11},{4,12},{5,13},{6,14},{7,15},{8,0},{9,1},... | collective-permute-start | bytes 1572872 | tf_op jit(solution)/shard_map/ppermute | solution.py:180
  165.7 11.6 %collective-permute-start.25 = (bf16[128,2048]{1,0:T(8,128)(2,1)S(1)}, bf16[128,2048]{1,0:T(8,128)(2,1)S(1)}, u32[]{:S(2)}, u32[]{:S(2)}) collective-permute-start(bf16[128,2048]{1,0:T(8,128)(2,1)S(1)} %add_convert_fusion.1), channel_id=1, source_target_pairs={{0,2},{1,3},{2,0},{3,1},{4,6},{5,7},{6,4},{7,5},{8,10},{9,11},{10,... | collective-permute-start | bytes 1572872 | tf_op jit(solution)/shard_map/ppermute | solution.py:180
